TPU v7x, 32 devices: a whole 2x2x4 slice. The times are simulated.
32 devices in a mesh: grp: 4 (over z), blk: 8 (over y, x, core).
Axes of the slice: x: 2, y: 2, z: 4, core: 2. Of those that a mesh axis runs over, the one named last changes fastest.
Arguments:
- pair_repr: bfloat16 [128, 128, 128], P(('grp', 'blk')), may hold values from -6 to 6
- pair_mask: int32 [128, 128], P(('grp', 'blk')), may hold values 0 or 1
- chain_index: int32 [128], replicated, may hold values from 0 to 3, never falling along the last dimension, each value on 1 to 64 neighbouring positions
- entity_embed: float32 [2, 128], replicated, may hold values from -3 to 3
- input_gain: float32 [2, 128], replicated, may hold values from 0.5 to 1.5
- input_bias: float32 [2, 128], replicated, may hold values from -2 to 2
- left_weight: bfloat16 [2, 128, 256], replicated, may hold values from -0.5 to 0.5
- right_weight: bfloat16 [2, 128, 256], replicated, may hold values from -0.5 to 0.5
- gate_weight: bfloat16 [2, 128, 128], replicated, may hold values from -0.5 to 0.5
- output_gain: float32 [2, 128], replicated, may hold values from 0.5 to 1.5
- output_bias: float32 [2, 128], replicated, may hold values from -2 to 2
- output_weight: bfloat16 [2, 128, 128], replicated, may hold values from -0.5 to 0.5
Outputs:
- pair_out: bfloat16 [128, 128, 128], P(('grp', 'blk'))
Inputs may be any that keep to these rules, and one draw needn't show every extreme that they name: `chain_index`: chain numbers never fall along the residues and every one of the 4 chains has at least one residue.
All inputs are finite; a program needn't handle non-finite values. No bound on the sum of `pair_mask` on one device may be relied on, other than what follows from the above.
Results may differ from a plain program's by a relative error of at most 0.0055.
Values may be sent and summed in bfloat16 or wider, within the bound.
No kernel may reach another device: no remote copies, remote signals or barrier semaphores. Data moves between devices by JAX's collectives and lax.ppermute only.
A program may use at most 64 MiB of HBM per device.

v0:
```python
import jax
import jax.numpy as jnp
from jax import lax
from jax.sharding import PartitionSpec as P


def normalize(values, gain_vector, bias_vector, along):
    average = jnp.mean(values, axis=along, keepdims=True)
    centered = values - average
    variance = jnp.mean(centered * centered, axis=along, keepdims=True)
    return centered * lax.rsqrt(variance + 1e-05) * gain_vector + bias_vector


def edge_values(normed, weight, mask_rows, hidden_count, row_count, columns):
    projected = lax.dot_general(
        weight, normed, (((0,), (1,)), ((), ())), preferred_element_type=jnp.float32
    )
    values = jax.nn.sigmoid(projected[:hidden_count]) * projected[hidden_count:] * mask_rows
    return values.astype(jnp.bfloat16).reshape(hidden_count, row_count, columns)


def to_planes(left_rows, right_rows, group_count, block_count):
    hidden_count, row_count, columns = left_rows.shape
    per_device = hidden_count // (group_count * block_count)
    shaped = (hidden_count, 1, row_count, columns)
    left_plane, right_plane = (
        lax.all_to_all(
            left_rows.reshape(shaped), ("grp", "blk"), split_axis=0, concat_axis=1, tiled=True
        ),
        lax.all_to_all(
            right_rows.reshape(shaped), ("grp", "blk"), split_axis=0, concat_axis=1, tiled=True
        ),
    )
    final = (per_device, group_count * block_count * row_count, columns)
    return (left_plane.reshape(final), right_plane.reshape(final))


def to_rows(product, group_count, block_count, row_count):
    per_device, total_rows, columns = product.shape
    shaped = product.reshape(1, per_device, group_count * block_count, row_count, columns)
    returned = lax.all_to_all(shaped, ("grp", "blk"), split_axis=2, concat_axis=0, tiled=True)
    return returned.reshape(-1, row_count * columns)


def shards(
    pair_repr,
    pair_mask,
    chain_index,
    entity_embed,
    input_gain,
    input_bias,
    left_weight,
    right_weight,
    gate_weight,
    output_gain,
    output_bias,
    output_weight,
):
    row_count, columns, channels = pair_repr.shape
    hidden_count = output_weight.shape[1]
    group_count = lax.axis_size("grp")
    block_count = lax.axis_size("blk")
    first_row = lax.axis_index(("grp", "blk")) * row_count
    own_chain = lax.dynamic_slice_in_dim(chain_index, first_row, row_count)
    same_chain = own_chain[:, None] == chain_index[None, :]
    current = pair_repr.astype(jnp.float32) + jnp.where(
        same_chain[:, :, None], entity_embed[1], entity_embed[0]
    )
    current = current.reshape(row_count * columns, channels)
    mask_rows = pair_mask.astype(jnp.float32).reshape(1, row_count * columns)
    contractions = [(((2,), (2,)), ((0,), (0,))), (((1,), (1,)), ((0,), (0,)))]
    stored = None
    for block_index in range(2):
        normed = normalize(current, input_gain[block_index], input_bias[block_index], 1).astype(
            jnp.bfloat16
        )
        left_rows = edge_values(
            normed, left_weight[block_index], mask_rows, hidden_count, row_count, columns
        )
        right_rows = edge_values(
            normed, right_weight[block_index], mask_rows, hidden_count, row_count, columns
        )
        gating = jax.nn.sigmoid(
            jnp.dot(normed, gate_weight[block_index], preferred_element_type=jnp.float32)
        )
        left_plane, right_plane = to_planes(left_rows, right_rows, group_count, block_count)
        product = lax.dot_general(
            left_plane, right_plane, contractions[block_index], preferred_element_type=jnp.float32
        ).astype(jnp.bfloat16)
        returned = to_rows(product, group_count, block_count, row_count).astype(jnp.float32)
        normed_out = normalize(
            returned, output_gain[block_index][:, None], output_bias[block_index][:, None], 0
        ).astype(jnp.bfloat16)
        update = lax.dot_general(
            normed_out,
            output_weight[block_index],
            (((0,), (0,)), ((), ())),
            preferred_element_type=jnp.float32,
        )
        stored = (current + gating * update).astype(jnp.bfloat16)
        current = lax.optimization_barrier(stored).astype(jnp.float32)
    return stored.reshape(row_count, columns, channels)


def solution(mesh):
    placed = (
        P(("grp", "blk"), None, None),
        P(("grp", "blk"), None),
        P(),
        P(),
        P(),
        P(),
        P(),
        P(),
        P(),
        P(),
        P(),
        P(),
    )
    return jax.shard_map(
        shards, mesh=mesh, in_specs=placed, out_specs=P(("grp", "blk"), None, None), check_vma=False
    )
```

profile of v0, /device:TPU:0, one launch (start us, length us, event | category | flops | bytes accessed | tf_op | source)
XLA Modules:
  0.0 84.5 jit_solution(17550164912926403626)
XLA Ops:
  0.0 0.8 dynamic_slice.3
  0.8 0.7 broadcast_compare_fusion
  1.5 0.8 slice_bitcast_fusion.5
  2.2 1.1 %fusion.56 = f32[4,128]{1,0:T(4,128)S(1)} fusion(f32[128]{0:T(128)S(1)} %get-tuple-element.20, f32[128]{0:T(128)S(1)} %get-tuple-element.19, pred[4,128]{1,0:T(4,128)(4,1)S(1)} %broadcast_compare_fusion, bf16[4,128,128]{2,1,0:T(8,128)(2,1)} %param.12), kind=kLoop, calls=%fused_computation.81 | loop fusion | flops 261632 | bytes 134656 | tf_op jit(solution)/shard_map/reduce_sum | solution.py:8
  3.4 0.3 multiply_reduce_fusion
  3.8 0.6 copy-done.5
  4.4 0.3 add_convert_fusion
  4.7 0.6 copy-done.2
  5.3 0.2 convolution_bitcast_fusion.2
  5.5 0.7 copy-done.1
  6.2 0.2 convolution_bitcast_fusion.3
  6.5 0.5 copy-done.4
  6.9 0.2 fusion.27
  7.1 0.8 copy.32
  7.9 7.3 %all-to-all-start = ((bf16[128,1,4,128]{3,2,1,0:T(4,128)(2,1)}), bf16[128,1,4,128]{3,2,1,0:T(4,128)(2,1)S(1)}, u32[]{:S(2)}, u32[]{:S(2)}) async-start(bf16[128,1,4,128]{3,2,1,0:T(4,128)(2,1)} %copy.32), calls=%async_computation | async-start | bytes 262144 | tf_op jit(solution)/shard_map/all_to_all | solution.py:27
  15.2 0.8 copy.35
  16.0 7.4 %all-to-all-done = bf16[128,1,4,128]{3,2,1,0:T(4,128)(2,1)S(1)} async-done(((bf16[128,1,4,128]{3,2,1,0:T(4,128)(2,1)}), bf16[128,1,4,128]{3,2,1,0:T(4,128)(2,1)S(1)}, u32[]{:S(2)}, u32[]{:S(2)}) %all-to-all-start) | async-done | bytes 131104 | tf_op jit(solution)/shard_map/all_to_all | solution.py:27
  23.4 2.6 %all-to-all-start.1 = ((bf16[128,1,4,128]{3,2,1,0:T(4,128)(2,1)}), bf16[128,1,4,128]{3,2,1,0:T(4,128)(2,1)S(1)}, u32[]{:S(2)}, u32[]{:S(2)}) async-start(bf16[128,1,4,128]{3,2,1,0:T(4,128)(2,1)} %copy.35), calls=%async_computation.1 | async-start | bytes 262144 | tf_op jit(solution)/shard_map/all_to_all | solution.py:30
  26.1 8.1 %all-to-all-done.1 = bf16[128,1,4,128]{3,2,1,0:T(4,128)(2,1)S(1)} async-done(((bf16[128,1,4,128]{3,2,1,0:T(4,128)(2,1)}), bf16[128,1,4,128]{3,2,1,0:T(4,128)(2,1)S(1)}, u32[]{:S(2)}, u32[]{:S(2)}) %all-to-all-start.1) | async-done | bytes 131104 | tf_op jit(solution)/shard_map/all_to_all | solution.py:30
  34.3 0.2 convolution_convert_fusion.1
  34.6 0.7 copy.38
  35.3 2.7 %all-to-all-start.2 = ((bf16[1,4,32,4,128]{4,3,1,0,2:T(4,128)(2,1)}), bf16[1,4,32,4,128]{4,3,1,0,2:T(4,128)(2,1)S(1)}, u32[]{:S(2)}, u32[]{:S(2)}) async-start(bf16[1,4,32,4,128]{4,3,1,0,2:T(4,128)(2,1)} %copy.38), calls=%async_computation.2 | async-start | bytes 262144 | tf_op jit(solution)/shard_map/all_to_all | solution.py:41
  38.3 0.2 fusion.7
  38.5 7.7 %all-to-all-done.2 = bf16[1,4,32,4,128]{4,3,1,0,2:T(4,128)(2,1)S(1)} async-done(((bf16[1,4,32,4,128]{4,3,1,0,2:T(4,128)(2,1)}), bf16[1,4,32,4,128]{4,3,1,0,2:T(4,128)(2,1)S(1)}, u32[]{:S(2)}, u32[]{:S(2)}) %all-to-all-start.2) | async-done | bytes 131104 | tf_op jit(solution)/shard_map/all_to_all | solution.py:41
  46.2 0.1 fusion.45
  46.3 0.1 fusion.48
  46.5 0.3 fusion.51
  46.9 0.5 copy-done.3
  47.3 0.2 fusion.8
  47.7 0.2 fusion.12
  47.9 0.3 convolution_bitcast_fusion.1
  48.3 0.3 convolution_bitcast_fusion
  48.6 0.2 fusion.17
  48.8 0.8 copy.39
  49.6 2.6 %all-to-all-start.3 = ((bf16[128,1,4,128]{3,2,1,0:T(4,128)(2,1)}), bf16[128,1,4,128]{3,2,1,0:T(4,128)(2,1)S(1)}, u32[]{:S(2)}, u32[]{:S(2)}) async-start(bf16[128,1,4,128]{3,2,1,0:T(4,128)(2,1)} %copy.39), calls=%async_computation.3 | async-start | bytes 262144 | tf_op jit(solution)/shard_map/all_to_all | solution.py:27
  52.2 0.8 copy.42
  52.9 7.4 %all-to-all-done.3 = bf16[128,1,4,128]{3,2,1,0:T(4,128)(2,1)S(1)} async-done(((bf16[128,1,4,128]{3,2,1,0:T(4,128)(2,1)}), bf16[128,1,4,128]{3,2,1,0:T(4,128)(2,1)S(1)}, u32[]{:S(2)}, u32[]{:S(2)}) %all-to-all-start.3) | async-done | bytes 131104 | tf_op jit(solution)/shard_map/all_to_all | solution.py:27
  60.4 2.6 %all-to-all-start.4 = ((bf16[128,1,4,128]{3,2,1,0:T(4,128)(2,1)}), bf16[128,1,4,128]{3,2,1,0:T(4,128)(2,1)S(1)}, u32[]{:S(2)}, u32[]{:S(2)}) async-start(bf16[128,1,4,128]{3,2,1,0:T(4,128)(2,1)} %copy.42), calls=%async_computation.4 | async-start | bytes 262144 | tf_op jit(solution)/shard_map/all_to_all | solution.py:30
  63.1 8.1 %all-to-all-done.4 = bf16[128,1,4,128]{3,2,1,0:T(4,128)(2,1)S(1)} async-done(((bf16[128,1,4,128]{3,2,1,0:T(4,128)(2,1)}), bf16[128,1,4,128]{3,2,1,0:T(4,128)(2,1)S(1)}, u32[]{:S(2)}, u32[]{:S(2)}) %all-to-all-start.4) | async-done | bytes 131104 | tf_op jit(solution)/shard_map/all_to_all | solution.py:30
  71.3 0.2 convolution_convert_fusion
  71.5 0.7 copy.46
  72.2 2.6 %all-to-all-start.5 = ((bf16[1,4,32,4,128]{4,3,1,0,2:T(4,128)(2,1)}), bf16[1,4,32,4,128]{4,3,1,0,2:T(4,128)(2,1)S(1)}, u32[]{:S(2)}, u32[]{:S(2)}) async-start(bf16[1,4,32,4,128]{4,3,1,0,2:T(4,128)(2,1)} %copy.46), calls=%async_computation.5 | async-start | bytes 262144 | tf_op jit(solution)/shard_map/all_to_all | solution.py:41
  75.0 0.3 fusion.4
  75.4 7.6 %all-to-all-done.5 = bf16[1,4,32,4,128]{4,3,1,0,2:T(4,128)(2,1)S(1)} async-done(((bf16[1,4,32,4,128]{4,3,1,0,2:T(4,128)(2,1)}), bf16[1,4,32,4,128]{4,3,1,0,2:T(4,128)(2,1)S(1)}, u32[]{:S(2)}, u32[]{:S(2)}) %all-to-all-start.5) | async-done | bytes 131104 | tf_op jit(solution)/shard_map/all_to_all | solution.py:41
  83.0 0.1 fusion.37
  83.2 0.1 fusion.40
  83.3 0.3 fusion.43
  83.7 0.9 %fusion.9 = bf16[512,128]{1,0:T(8,128)(2,1)} fusion(f32[512,128]{1,0:T(8,128)S(1)} %fusion.4, bf16[512,128]{1,0:T(8,128)(2,1)S(1)} %fusion.8, bf16[16,8,4,128]{3,2,1,0:T(4,128)(2,1)S(1)} %bitcast.151, bf16[2,128,128]{2,1,0:T(8,128)(2,1)S(1)} %copy-done.3), kind=kOutput, calls=%fused_computation.17 | convolution fusion | flops 17039360 | bytes 688128 | tf_op jit(solution)/shard_map/dot_general | solution.py:94
  (39 shorter events, 1.1 us)
Async XLA Ops:
  0.0 3.4 %copy-start = (bf16[4,128,128]{2,1,0:T(8,128)(2,1)S(1)}, bf16[4,128,128]{2,1,0:T(8,128)(2,1)}, u32[]{:S(2)}) copy-start(bf16[4,128,128]{2,1,0:T(8,128)(2,1)} %param.12) | copy-start | bytes 393220
  3.7 0.7 copy-start.5
  3.7 0.7 copy-start.6
  4.4 0.9 %copy-start.2 = (bf16[2,128,256]{2,1,0:T(8,128)(2,1)S(1)}, bf16[2,128,256]{2,1,0:T(8,128)(2,1)}, u32[]{:S(2)}) copy-start(bf16[2,128,256]{2,1,0:T(8,128)(2,1)} %param.19) | copy-start | bytes 393220
  5.3 0.9 %copy-start.1 = (bf16[2,128,256]{2,1,0:T(8,128)(2,1)S(1)}, bf16[2,128,256]{2,1,0:T(8,128)(2,1)}, u32[]{:S(2)}) copy-start(bf16[2,128,256]{2,1,0:T(8,128)(2,1)} %param.18) | copy-start | bytes 393220
  6.2 0.7 copy-start.4
  7.9 15.5 %all-to-all-start = ((bf16[128,1,4,128]{3,2,1,0:T(4,128)(2,1)}), bf16[128,1,4,128]{3,2,1,0:T(4,128)(2,1)S(1)}, u32[]{:S(2)}, u32[]{:S(2)}) async-start(bf16[128,1,4,128]{3,2,1,0:T(4,128)(2,1)} %copy.32), calls=%async_computation | async-start | bytes 262144 | tf_op jit(solution)/shard_map/all_to_all | solution.py:27
  23.4 10.8 %all-to-all-start.1 = ((bf16[128,1,4,128]{3,2,1,0:T(4,128)(2,1)}), bf16[128,1,4,128]{3,2,1,0:T(4,128)(2,1)S(1)}, u32[]{:S(2)}, u32[]{:S(2)}) async-start(bf16[128,1,4,128]{3,2,1,0:T(4,128)(2,1)} %copy.35), calls=%async_computation.1 | async-start | bytes 262144 | tf_op jit(solution)/shard_map/all_to_all | solution.py:30
  35.3 2.7 %copy-start.7 = (f32[2,128]{1,0:T(2,128)S(1)}, f32[2,128]{1,0:T(2,128)}, u32[]{:S(2)}) copy-start(f32[2,128]{1,0:T(2,128)} %param.22) | copy-start | bytes 3076
  35.3 2.7 %copy-start.8 = (f32[2,128]{1,0:T(2,128)S(1)}, f32[2,128]{1,0:T(2,128)}, u32[]{:S(2)}) copy-start(f32[2,128]{1,0:T(2,128)} %param.21) | copy-start | bytes 3076
  35.3 3.0 %copy-start.9 = (bf16[2,128,128]{2,1,0:T(8,128)(2,1)S(1)}, bf16[2,128,128]{2,1,0:T(8,128)(2,1)}, u32[]{:S(2)}) copy-start(bf16[2,128,128]{2,1,0:T(8,128)(2,1)} %param.20) | copy-start | bytes 196612
  35.3 10.9 %all-to-all-start.2 = ((bf16[1,4,32,4,128]{4,3,1,0,2:T(4,128)(2,1)}), bf16[1,4,32,4,128]{4,3,1,0,2:T(4,128)(2,1)S(1)}, u32[]{:S(2)}, u32[]{:S(2)}) async-start(bf16[1,4,32,4,128]{4,3,1,0,2:T(4,128)(2,1)} %copy.38), calls=%async_computation.2 | async-start | bytes 262144 | tf_op jit(solution)/shard_map/all_to_all | solution.py:41
  46.5 0.8 copy-start.3
  49.6 10.8 %all-to-all-start.3 = ((bf16[128,1,4,128]{3,2,1,0:T(4,128)(2,1)}), bf16[128,1,4,128]{3,2,1,0:T(4,128)(2,1)S(1)}, u32[]{:S(2)}, u32[]{:S(2)}) async-start(bf16[128,1,4,128]{3,2,1,0:T(4,128)(2,1)} %copy.39), calls=%async_computation.3 | async-start | bytes 262144 | tf_op jit(solution)/shard_map/all_to_all | solution.py:27
  60.4 10.8 %all-to-all-start.4 = ((bf16[128,1,4,128]{3,2,1,0:T(4,128)(2,1)}), bf16[128,1,4,128]{3,2,1,0:T(4,128)(2,1)S(1)}, u32[]{:S(2)}, u32[]{:S(2)}) async-start(bf16[128,1,4,128]{3,2,1,0:T(4,128)(2,1)} %copy.42), calls=%async_computation.4 | async-start | bytes 262144 | tf_op jit(solution)/shard_map/all_to_all | solution.py:30
  72.2 10.8 %all-to-all-start.5 = ((bf16[1,4,32,4,128]{4,3,1,0,2:T(4,128)(2,1)}), bf16[1,4,32,4,128]{4,3,1,0,2:T(4,128)(2,1)S(1)}, u32[]{:S(2)}, u32[]{:S(2)}) async-start(bf16[1,4,32,4,128]{4,3,1,0,2:T(4,128)(2,1)} %copy.46), calls=%async_computation.5 | async-start | bytes 262144 | tf_op jit(solution)/shard_map/all_to_all | solution.py:41
where the time goes:
time: 85.2 us; the launch traced here: 84.5 us
  waiting for transfers between devices  46.4 us (54%)
  starting transfers between devices  20.3 us (24%)
  local copies, waits for them, and re-layouts  9.94 us (12%)
  other arithmetic  4.47 us (5%)
  matrix products  3.15 us (4%)
    all_to_all x2, waiting for transfers between devices, to_planes(): lax.all_to_all(right_rows.reshape(shaped), ('grp', 'blk'), split_axis=0,...  16.1 us
    all_to_all x2, waiting for transfers between devices, to_rows(): lax.all_to_all(shaped, ('grp', 'blk'), split_axis=2, concat_axis=0, tiled...  15.4 us
    all_to_all x2, waiting for transfers between devices, to_planes(): lax.all_to_all(left_rows.reshape(shaped), ('grp', 'blk'), split_axis=0, c...  14.9 us
    all_to_all x2, starting transfers between devices, to_planes(): lax.all_to_all(left_rows.reshape(shaped), ('grp', 'blk'), split_axis=0, c...  9.9 us
    all_to_all x2, starting transfers between devices, to_rows(): lax.all_to_all(shaped, ('grp', 'blk'), split_axis=2, concat_axis=0, tiled...  5.28 us
    all_to_all x2, starting transfers between devices, to_planes(): lax.all_to_all(right_rows.reshape(shaped), ('grp', 'blk'), split_axis=0,...  5.14 us
    unnamed x20, local copies, waits for them, and re-layouts  2.98 us
  transfers between devices with their start and end apart: 6, of which 6 were waited for; matrix products, arithmetic and copies ran while one was open for 3% of the time, Pallas kernels for 0%

commit v1 on v0

--- a/solution.py
+++ b/solution.py
@@ -21,18 +21,15 @@
 
 def to_planes(left_rows, right_rows, group_count, block_count):
     hidden_count, row_count, columns = left_rows.shape
-    per_device = hidden_count // (group_count * block_count)
-    shaped = (hidden_count, 1, row_count, columns)
-    left_plane, right_plane = (
-        lax.all_to_all(
-            left_rows.reshape(shaped), ("grp", "blk"), split_axis=0, concat_axis=1, tiled=True
-        ),
-        lax.all_to_all(
-            right_rows.reshape(shaped), ("grp", "blk"), split_axis=0, concat_axis=1, tiled=True
-        ),
+    devices = group_count * block_count
+    per_device = hidden_count // devices
+    both = jnp.stack([left_rows, right_rows], axis=1).reshape(
+        devices, per_device * 2 * row_count, columns
     )
-    final = (per_device, group_count * block_count * row_count, columns)
-    return (left_plane.reshape(final), right_plane.reshape(final))
+    moved = lax.all_to_all(both, ("grp", "blk"), split_axis=0, concat_axis=0, tiled=True)
+    planes = moved.reshape(devices, per_device, 2, row_count, columns).transpose(2, 1, 0, 3, 4)
+    planes = planes.reshape(2, per_device, devices * row_count, columns)
+    return planes[0], planes[1]
 
 
 def to_rows(product, group_count, block_count, row_count):

time: 85.2 us -> 66.8 us (0.78)
  waiting for transfers between devices: 46.4 us -> 15.4 us
  blocking collectives: 0 us -> 30 us
  starting transfers between devices: 20.3 us -> 5.28 us
  local copies, waits for them, and re-layouts: 9.94 us -> 7.41 us
    all_to_all x4 -> x0, waiting for transfers between devices: 31 us -> none  [the longest x2 16.1 us: to_planes(): lax.all_to_all(right_rows.reshape(shaped), ('grp', 'blk'), split_axis=0,...]
    all_to_all x0 -> x2, blocking collectives: none -> 30 us  [to_planes(): lax.all_to_all(both, ('grp', 'blk'), split_axis=0, concat_axis=0, tiled=T...]
    all_to_all x4 -> x0, starting transfers between devices: 15 us -> none  [the longest x2 9.9 us: to_planes(): lax.all_to_all(left_rows.reshape(shaped), ('grp', 'blk'), split_axis=0, c...]
    another operation x4, local copies, waits for them, and re-layouts: 3.12 us -> 0.57 us  [to_planes(): jnp.stack([left_rows, right_rows], axis=1)]
  transfers between devices with their start and end apart: 6 -> 2, of which waited for: 6 -> 2; matrix products, arithmetic and copies ran while one was open for 3% -> 1% of each run, Pallas kernels for 0% -> 0%
where the time goes in v1:
time: 66.8 us; the launch traced here: 66.4 us
  blocking collectives  30 us (45%)
  waiting for transfers between devices  15.4 us (23%)
  local copies, waits for them, and re-layouts  7.41 us (11%)
  starting transfers between devices  5.28 us (8%)
  other arithmetic  4.85 us (7%)
  matrix products  3.14 us (5%)
    all_to_all x2, blocking collectives, to_planes(): lax.all_to_all(both, ('grp', 'blk'), split_axis=0, concat_axis=0, tiled=T...  30 us
    all_to_all x2, waiting for transfers between devices, to_rows(): lax.all_to_all(shaped, ('grp', 'blk'), split_axis=2, concat_axis=0, tiled...  15.4 us
    all_to_all x2, starting transfers between devices, to_rows(): lax.all_to_all(shaped, ('grp', 'blk'), split_axis=2, concat_axis=0, tiled...  5.28 us
    unnamed x20, local copies, waits for them, and re-layouts  2.98 us
    reduce_sum x4, other arithmetic, normalize(): average = jnp.mean(values, axis=along, keepdims=True)  1.55 us
    reshape x2, local copies, waits for them, and re-layouts, to_rows(): product.reshape(1, per_device, group_count * block_count, row_count, colu...  1.4 us
  transfers between devices with their start and end apart: 2, of which 2 were waited for; matrix products, arithmetic and copies ran while one was open for 1% of the time, Pallas kernels for 0%

profile of v1, /device:TPU:0, one launch (start us, length us, event | category | flops | bytes accessed | tf_op | source)
XLA Modules:
  0.0 66.4 jit_solution(985036082120588981)
XLA Ops:
  0.0 0.8 %dynamic_slice.3 = s32[4]{0:T(128)S(1)} dynamic-slice(s32[128]{0:T(128)} %param.14, s32[]{:T(128)S(6)} %select_n.7), dynamic_slice_sizes={4} | dynamic-slice | bytes 36 | tf_op jit(solution)/shard_map/dynamic_slice | solution.py:61
  0.8 0.7 %broadcast_compare_fusion = pred[4,128]{1,0:T(4,128)(4,1)S(1)} fusion(s32[128]{0:T(128)} %param.14, s32[4]{0:T(128)S(1)} %dynamic_slice.3), kind=kLoop, calls=%fused_computation.109 | loop fusion | flops 512 | bytes 1040 | tf_op jit(solution)/shard_map/eq | solution.py:62
  1.5 0.8 %slice_bitcast_fusion.5 = (f32[128]{0:T(128)S(1)}, f32[128]{0:T(128)S(1)}) fusion(f32[2,128]{1,0:T(2,128)} %param.15), kind=kLoop, calls=%fused_computation.119 | loop fusion | bytes 2048 | tf_op jit(solution)/shard_map/squeeze | solution.py:64
  2.2 1.1 %fusion.56 = f32[4,128]{1,0:T(4,128)S(1)} fusion(f32[128]{0:T(128)S(1)} %get-tuple-element.24, f32[128]{0:T(128)S(1)} %get-tuple-element.23, pred[4,128]{1,0:T(4,128)(4,1)S(1)} %broadcast_compare_fusion, bf16[4,128,128]{2,1,0:T(8,128)(2,1)} %param.12), kind=kLoop, calls=%fused_computation.83 | loop fusion | flops 261632 | bytes 134656 | tf_op jit(solution)/shard_map/reduce_sum | solution.py:8
  3.4 0.3 multiply_reduce_fusion
  3.8 0.6 copy-done.5
  4.4 0.3 add_convert_fusion
  4.7 0.6 copy-done.1
  5.3 0.2 convolution_bitcast_fusion.2
  5.5 0.7 %copy-done.2 = bf16[2,128,256]{2,1,0:T(8,128)(2,1)S(1)} copy-done((bf16[2,128,256]{2,1,0:T(8,128)(2,1)S(1)}, bf16[2,128,256]{2,1,0:T(8,128)(2,1)}, u32[]{:S(2)}) %copy-start.2) | copy-done | bytes 131096
  6.2 0.2 convolution_bitcast_fusion.3
  6.5 0.5 copy-done.4
  6.9 0.2 fusion.32
  7.1 0.1 copy.31
  7.3 0.1 copy.32
  7.4 0.2 pad_maximum_fusion
  7.6 17.7 %all_to_all.28 = bf16[32,32,128]{2,1,0:T(8,128)(2,1)S(1)} all-to-all(bf16[32,32,128]{2,1,0:T(8,128)(2,1)S(1)} %bitcast.138), channel_id=1, replica_groups=mesh['grp'=4,'blk'=8] {'grp','blk'}, dimensions={0} | all-to-all | bytes 524288 | tf_op jit(solution)/shard_map/all_to_all | solution.py:29
  25.3 0.1 copy.33
  25.6 0.2 convolution_convert_fusion.1
  25.8 0.7 %copy.36 = bf16[1,4,32,4,128]{4,3,1,0,2:T(4,128)(2,1)} copy(bf16[1,4,32,4,128]{4,3,2,1,0:T(4,128)(2,1)S(1)} %bitcast.148) | data formatting | bytes 262144 | tf_op jit(solution)/shard_map/reshape | solution.py:37
  26.5 2.7 %all-to-all-start.1 = ((bf16[1,4,32,4,128]{4,3,1,0,2:T(4,128)(2,1)}), bf16[1,4,32,4,128]{4,3,1,0,2:T(4,128)(2,1)S(1)}, u32[]{:S(2)}, u32[]{:S(2)}) async-start(bf16[1,4,32,4,128]{4,3,1,0,2:T(4,128)(2,1)} %copy.36), calls=%async_computation.1 | async-start | bytes 262144 | tf_op jit(solution)/shard_map/all_to_all | solution.py:38
  29.4 0.1 mul.166
  29.5 0.2 fusion.7
  29.7 7.7 %all-to-all-done.1 = bf16[1,4,32,4,128]{4,3,1,0,2:T(4,128)(2,1)S(1)} async-done(((bf16[1,4,32,4,128]{4,3,1,0,2:T(4,128)(2,1)}), bf16[1,4,32,4,128]{4,3,1,0,2:T(4,128)(2,1)S(1)}, u32[]{:S(2)}, u32[]{:S(2)}) %all-to-all-start.1) | async-done | bytes 131104 | tf_op jit(solution)/shard_map/all_to_all | solution.py:38
  37.4 0.1 fusion.45
  37.6 0.1 fusion.48
  37.8 0.3 fusion.51
  38.1 0.5 copy-done.3
  38.6 0.2 fusion.8
  38.8 0.1 convert_reduce_fusion
  38.9 0.2 fusion.12
  39.2 0.3 convolution_bitcast_fusion
  39.5 0.3 convolution_bitcast_fusion.1
  39.8 0.2 fusion.22
  40.0 0.1 copy.37
  40.2 0.1 copy.38
  40.3 0.2 pad_maximum_fusion.1
  40.5 12.3 %all_to_all.29 = bf16[32,32,128]{2,1,0:T(8,128)(2,1)S(1)} all-to-all(bf16[32,32,128]{2,1,0:T(8,128)(2,1)S(1)} %bitcast.139), channel_id=1, replica_groups=mesh['grp'=4,'blk'=8] {'grp','blk'}, dimensions={0} | all-to-all | bytes 524288 | tf_op jit(solution)/shard_map/all_to_all | solution.py:29
  52.8 0.1 copy.39
  53.1 0.2 convolution_convert_fusion
  53.3 0.7 %copy.43 = bf16[1,4,32,4,128]{4,3,1,0,2:T(4,128)(2,1)} copy(bf16[1,4,32,4,128]{4,3,2,1,0:T(4,128)(2,1)S(1)} %bitcast.150) | data formatting | bytes 262144 | tf_op jit(solution)/shard_map/reshape | solution.py:37
  54.0 2.6 %all-to-all-start.3 = ((bf16[1,4,32,4,128]{4,3,1,0,2:T(4,128)(2,1)}), bf16[1,4,32,4,128]{4,3,1,0,2:T(4,128)(2,1)S(1)}, u32[]{:S(2)}, u32[]{:S(2)}) async-start(bf16[1,4,32,4,128]{4,3,1,0,2:T(4,128)(2,1)} %copy.43), calls=%async_computation.3 | async-start | bytes 262144 | tf_op jit(solution)/shard_map/all_to_all | solution.py:38
  56.8 0.3 fusion.4
  57.2 7.6 %all-to-all-done.3 = bf16[1,4,32,4,128]{4,3,1,0,2:T(4,128)(2,1)S(1)} async-done(((bf16[1,4,32,4,128]{4,3,1,0,2:T(4,128)(2,1)}), bf16[1,4,32,4,128]{4,3,1,0,2:T(4,128)(2,1)S(1)}, u32[]{:S(2)}, u32[]{:S(2)}) %all-to-all-start.3) | async-done | bytes 131104 | tf_op jit(solution)/shard_map/all_to_all | solution.py:38
  64.8 0.1 fusion.37
  65.0 0.1 fusion.40
  65.1 0.3 fusion.43
  65.5 0.9 %fusion.9 = bf16[512,128]{1,0:T(8,128)(2,1)} fusion(f32[512,128]{1,0:T(8,128)S(1)} %fusion.4, bf16[512,128]{1,0:T(8,128)(2,1)S(1)} %fusion.8, bf16[16,8,4,128]{3,2,1,0:T(4,128)(2,1)S(1)} %bitcast.151, bf16[2,128,128]{2,1,0:T(8,128)(2,1)S(1)} %copy-done.3), kind=kOutput, calls=%fused_computation.17 | convolution fusion | flops 17039360 | bytes 688128 | tf_op jit(solution)/shard_map/dot_general | solution.py:91
  (35 shorter events, 0.7 us)
Async XLA Ops:
  0.0 3.4 %copy-start = (bf16[4,128,128]{2,1,0:T(8,128)(2,1)S(1)}, bf16[4,128,128]{2,1,0:T(8,128)(2,1)}, u32[]{:S(2)}) copy-start(bf16[4,128,128]{2,1,0:T(8,128)(2,1)} %param.12) | copy-start | bytes 393220
  3.7 0.7 %copy-start.5 = (f32[2,128]{1,0:T(2,128)S(1)}, f32[2,128]{1,0:T(2,128)}, u32[]{:S(2)}) copy-start(f32[2,128]{1,0:T(2,128)} %param.17) | copy-start | bytes 3076
  3.7 0.7 %copy-start.6 = (f32[2,128]{1,0:T(2,128)S(1)}, f32[2,128]{1,0:T(2,128)}, u32[]{:S(2)}) copy-start(f32[2,128]{1,0:T(2,128)} %param.16) | copy-start | bytes 3076
  4.4 0.9 %copy-start.1 = (bf16[2,128,256]{2,1,0:T(8,128)(2,1)S(1)}, bf16[2,128,256]{2,1,0:T(8,128)(2,1)}, u32[]{:S(2)}) copy-start(bf16[2,128,256]{2,1,0:T(8,128)(2,1)} %param.19) | copy-start | bytes 393220
  5.3 0.9 %copy-start.2 = (bf16[2,128,256]{2,1,0:T(8,128)(2,1)S(1)}, bf16[2,128,256]{2,1,0:T(8,128)(2,1)}, u32[]{:S(2)}) copy-start(bf16[2,128,256]{2,1,0:T(8,128)(2,1)} %param.18) | copy-start | bytes 393220
  6.2 0.7 %copy-start.4 = (s32[4,128]{1,0:T(4,128)S(1)}, s32[4,128]{1,0:T(4,128)}, u32[]{:S(2)}) copy-start(s32[4,128]{1,0:T(4,128)} %param.13) | copy-start | bytes 6148
  26.5 2.7 %copy-start.7 = (f32[2,128]{1,0:T(2,128)S(1)}, f32[2,128]{1,0:T(2,128)}, u32[]{:S(2)}) copy-start(f32[2,128]{1,0:T(2,128)} %param.22) | copy-start | bytes 3076
  26.5 2.7 %copy-start.8 = (f32[2,128]{1,0:T(2,128)S(1)}, f32[2,128]{1,0:T(2,128)}, u32[]{:S(2)}) copy-start(f32[2,128]{1,0:T(2,128)} %param.21) | copy-start | bytes 3076
  26.5 3.0 %copy-start.9 = (bf16[2,128,128]{2,1,0:T(8,128)(2,1)S(1)}, bf16[2,128,128]{2,1,0:T(8,128)(2,1)}, u32[]{:S(2)}) copy-start(bf16[2,128,128]{2,1,0:T(8,128)(2,1)} %param.20) | copy-start | bytes 196612
  26.5 10.9 %all-to-all-start.1 = ((bf16[1,4,32,4,128]{4,3,1,0,2:T(4,128)(2,1)}), bf16[1,4,32,4,128]{4,3,1,0,2:T(4,128)(2,1)S(1)}, u32[]{:S(2)}, u32[]{:S(2)}) async-start(bf16[1,4,32,4,128]{4,3,1,0,2:T(4,128)(2,1)} %copy.36), calls=%async_computation.1 | async-start | bytes 262144 | tf_op jit(solution)/shard_map/all_to_all | solution.py:38
  37.7 0.8 %copy-start.3 = (bf16[2,128,128]{2,1,0:T(8,128)(2,1)S(1)}, bf16[2,128,128]{2,1,0:T(8,128)(2,1)}, u32[]{:S(2)}) copy-start(bf16[2,128,128]{2,1,0:T(8,128)(2,1)} %param.23) | copy-start | bytes 196612
  54.0 10.8 %all-to-all-start.3 = ((bf16[1,4,32,4,128]{4,3,1,0,2:T(4,128)(2,1)}), bf16[1,4,32,4,128]{4,3,1,0,2:T(4,128)(2,1)S(1)}, u32[]{:S(2)}, u32[]{:S(2)}) async-start(bf16[1,4,32,4,128]{4,3,1,0,2:T(4,128)(2,1)} %copy.43), calls=%async_computation.3 | async-start | bytes 262144 | tf_op jit(solution)/shard_map/all_to_all | solution.py:38

commit v2 on v1

v2 whole, which is shorter than its diff:
```python
import functools

import jax
import jax.numpy as jnp
from jax import lax
from jax.experimental import pallas as pl
from jax.experimental.pallas import tpu as pltpu
from jax.sharding import PartitionSpec as P

AXES = ("grp", "blk")
F32, BF16 = jnp.float32, jnp.bfloat16
ON_SUBLANES = (((0,), (0,)), ((), ()))
ON_LANES = (((1,), (1,)), ((), ()))
LANES = 128


def unit(size):
    down = lax.broadcasted_iota(jnp.int32, (size, size), 0)
    across = lax.broadcasted_iota(jnp.int32, (size, size), 1)
    return jnp.where(down == across, 1.0, 0.0).astype(BF16)


def as_columns(rows_ref, *rows):
    rows_ref[...] = jnp.zeros(rows_ref.shape, F32)
    for place, row in enumerate(rows):
        rows_ref[place : place + 1, :] = row
    turned = jnp.transpose(rows_ref[...])
    return [turned[:, place : place + 1] for place in range(len(rows))]


def normalize(values, gain, bias):
    average = jnp.mean(values, axis=0, keepdims=True)
    centered = values - average
    variance = jnp.mean(centered * centered, axis=0, keepdims=True)
    return centered * lax.rsqrt(variance + 1e-05) * gain + bias


def put(ref, first, count, stride, values):
    for part in range(ref.shape[0]):
        at = part * LANES
        ref[part, pl.ds(first, count, stride=stride), :] = values[:, at : at + LANES]


def take(ref, first, count, stride):
    rows = pl.ds(first, count, stride=stride)
    return jnp.concatenate([ref[part, rows, :] for part in range(ref.shape[0])], axis=1)


def widen(source, ref):
    for part in range(ref.shape[0]):
        ref[part] = source[:, part * LANES : (part + 1) * LANES].astype(F32)


def pack(ref, out):
    for part in range(ref.shape[0]):
        out[:, part * LANES : (part + 1) * LANES] = ref[part].astype(BF16)


def edges(normed_ref, sides, mask_ref, e32, out_ref):
    row_count, columns = mask_ref.shape
    hidden = e32.shape[1] // (2 * row_count)
    for row in range(row_count):
        lanes = pl.ds(row * columns, columns)
        mask = mask_ref[row : row + 1, :]
        for side, weight in enumerate(sides):
            projected = lax.dot_general(
                weight, normed_ref[:, lanes], ON_SUBLANES, preferred_element_type=F32
            )
            values = jax.nn.sigmoid(projected[:hidden]) * projected[hidden:] * mask
            put(e32, side * row_count + row, hidden, 2 * row_count, values)
    pack(e32, out_ref)


def gates(normed_ref, weight, out_ref):
    out_ref[...] = jax.nn.sigmoid(
        lax.dot_general(weight, normed_ref[...], ON_SUBLANES, preferred_element_type=F32)
    )


def start_kernel(
    pair_h, mask_h, chain_h, embed_h, gain_h, bias_h, gain_oh, bias_oh, left_h, right_h, gate_h,
    out, state, gating, mask_out, columns_out,
    pair, mask, chain, embed, gain, bias, gain_o, bias_o, left, right, gate,
    e32, normed, rows, arrived,
):
    moves = [
        pltpu.make_async_copy(source, target, arrived.at[place])
        for place, (source, target) in enumerate(
            [
                (pair_h, pair),
                (chain_h, chain),
                (embed_h, embed),
                (gain_h, gain),
                (bias_h, bias),
                (gain_oh, gain_o),
                (bias_oh, bias_o),
                (left_h.at[0], left),
                (mask_h, mask),
                (right_h.at[0], right),
                (gate_h.at[0], gate),
            ]
        )
    ]
    for move in moves:
        move.start()
    row_count, columns, channels = pair.shape
    first = lax.axis_index(AXES) * row_count
    one = unit(channels)
    for move in moves[1:7]:
        move.wait()
    other, same, gain_c, bias_c = as_columns(
        rows, embed[0:1, :], embed[1:2, :], gain[0:1, :], bias[0:1, :]
    )
    rows[0:8, :] = jnp.concatenate([gain_o[...], bias_o[...], gain[...], bias[...]])
    columns_out[...] = jnp.transpose(rows[...])
    chains = jnp.broadcast_to(chain[...].astype(F32), (row_count, chain.shape[1]))
    place = lax.broadcasted_iota(jnp.int32, chains.shape, 1)
    mine = first + lax.broadcasted_iota(jnp.int32, chains.shape, 0)
    own = jnp.sum(jnp.where(place == mine, chains, 0.0), axis=1, keepdims=True)
    alike = jnp.where(chains == own, 1.0, 0.0)
    moves[0].wait()
    for row in range(row_count):
        lanes = pl.ds(row * columns, columns)
        turned = lax.dot_general(one, pair[row], ON_LANES, preferred_element_type=F32)
        hit = jnp.broadcast_to(alike[row : row + 1, :], turned.shape) > 0.5
        values = turned + jnp.where(hit, same, other)
        state[:, lanes] = values
        normed[:, lanes] = normalize(values, gain_c, bias_c).astype(BF16)
    for move in moves[7:]:
        move.wait()
    mask_out[...] = mask[...].astype(F32)
    edges(normed, (left[...], right[...]), mask_out, e32, out)
    gates(normed, gate[...], gating)


def product_kernel(incoming, devices, x, out, x32, t32, o32):
    columns = x.shape[1]
    row_count = columns // devices
    per_device = x.shape[0] // (2 * columns)
    widen(x, x32)
    apart = per_device * 2 * row_count

    def block(channel, side, row):
        return take(x32, channel * 2 * row_count + side * row_count + row, devices, apart)

    for channel in range(per_device):
        left = jnp.concatenate([block(channel, 0, r) for r in range(row_count)]).astype(BF16)
        if incoming:
            right = jnp.concatenate([block(channel, 1, r) for r in range(row_count)])
            product = lax.dot_general(
                left, right.astype(BF16), ON_SUBLANES, preferred_element_type=F32
            )
            put(t32, 0, columns, 1, product)
            pieces = [take(t32, r, devices, row_count) for r in range(row_count)]
        else:
            for r in range(row_count):
                put(t32, r, devices, row_count, block(channel, 1, r))
            right = take(t32, 0, columns, 1).astype(BF16)
            product = lax.dot_general(left, right, ON_LANES, preferred_element_type=F32)
            pieces = [product[r * devices : (r + 1) * devices] for r in range(row_count)]
        for r in range(row_count):
            put(o32, channel * row_count + r, devices, per_device * row_count, pieces[r])
    pack(o32, out)


def finish(y, y32, normed, gain_c, bias_c, weight, columns):
    hidden, positions = normed.shape
    row_count = positions // columns
    widen(y, y32)
    for row in range(row_count):
        values = take(y32, row, hidden, row_count)
        normed[:, pl.ds(row * columns, columns)] = normalize(values, gain_c, bias_c).astype(BF16)
    return lax.dot_general(weight, normed[...], ON_SUBLANES, preferred_element_type=F32)


def middle_kernel(
    y, state, gating, mask, turned, weight_o, left, right, gate,
    out, state_out, gating_out, y32, e32, normed,
):
    row_count, columns = mask.shape
    update = finish(y, y32, normed, turned[:, 0:1], turned[:, 2:3], weight_o[0], columns)
    state_out[...] = (state[...] + gating[...] * update).astype(BF16)
    for row in range(row_count):
        lanes = pl.ds(row * columns, columns)
        values = state_out[:, lanes].astype(F32)
        normed[:, lanes] = normalize(values, turned[:, 5:6], turned[:, 7:8]).astype(BF16)
    edges(normed, (left[1], right[1]), mask, e32, out)
    gates(normed, gate[1], gating_out)


def end_kernel(y, state, gating, turned, weight_o, out, y32, normed, ready, sent):
    row_count, columns, channels = out.shape
    update = finish(y, y32, normed, turned[:, 1:2], turned[:, 3:4], weight_o[1], columns)
    stored = (state[...].astype(F32) + gating[...] * update).astype(BF16)
    one = unit(LANES)
    moves = []
    for row in range(row_count):
        for part in range(columns // LANES):
            at = row * columns + part * LANES
            flat = lax.dot_general(
                one, stored[:, at : at + LANES], ON_LANES, preferred_element_type=F32
            )
            ready[row, pl.ds(part * LANES, LANES), :] = flat.astype(BF16)
        moves.append(pltpu.make_async_copy(ready.at[row], out.at[row], sent.at[row]))
        moves[-1].start()
    for move in moves:
        move.wait()


def call(kernel, shapes, scratch, semaphores=0, far_in=False, far_out=False):
    near = pl.BlockSpec(memory_space=pltpu.VMEM)
    far = pl.BlockSpec(memory_space=pltpu.HBM)

    def run(*operands):
        if far_in:
            operands = [pltpu.with_memory_space_constraint(o, pltpu.HBM) for o in operands]
        return pl.pallas_call(
            kernel,
            out_shape=[jax.ShapeDtypeStruct(*s) for s in shapes],
            in_specs=[far if far_in else near] * len(operands),
            out_specs=[far if far_out else near] * len(shapes),
            scratch_shapes=[pltpu.VMEM(*s) for s in scratch]
            + [pltpu.SemaphoreType.DMA((semaphores,))] * (semaphores > 0),
            compiler_params=pltpu.CompilerParams(vmem_limit_bytes=16 << 20),
        )(*operands)

    return run


def exchange(rows):
    devices = lax.axis_size(AXES[0]) * lax.axis_size(AXES[1])
    count, columns = rows.shape
    moved = lax.all_to_all(
        rows.reshape(devices, count // devices, columns),
        AXES,
        split_axis=0,
        concat_axis=0,
        tiled=True,
    )
    return moved.reshape(count, columns)


def shards(
    pair_repr,
    pair_mask,
    chain_index,
    entity_embed,
    input_gain,
    input_bias,
    left_weight,
    right_weight,
    gate_weight,
    output_gain,
    output_bias,
    output_weight,
):
    row_count, columns, channels = pair_repr.shape
    hidden = output_weight.shape[1]
    devices = lax.axis_size(AXES[0]) * lax.axis_size(AXES[1])
    positions = row_count * columns
    edge = (hidden * 2 * row_count, columns)
    prod = (hidden * row_count, columns)
    wide = (channels, positions)

    def tall(shape):
        return ((shape[1] // LANES, shape[0], LANES), F32)

    columnar = ((channels, 8), F32)
    weights = [left_weight.shape[1:], right_weight.shape[1:], gate_weight.shape[1:]]

    sent, state, gating, mask, turned = call(
        start_kernel,
        [(edge, BF16), (wide, F32), (wide, F32), (pair_mask.shape, F32), columnar],
        [(pair_repr.shape, BF16), (pair_mask.shape, jnp.int32), ((1, columns), jnp.int32)]
        + [((2, channels), F32)] * 5
        + [(shape, BF16) for shape in weights]
        + [tall(edge), (wide, BF16), ((8, channels), F32)],
        semaphores=11,
        far_in=True,
    )(
        pair_repr, pair_mask, chain_index.reshape(1, -1), entity_embed, input_gain, input_bias,
        output_gain, output_bias, left_weight, right_weight, gate_weight,
    )

    def product(rows, incoming):
        return call(
            functools.partial(product_kernel, incoming, devices),
            [(prod, BF16)],
            [tall(edge), tall((columns, columns)), tall(prod)],
        )(rows)[0]

    back = exchange(product(exchange(sent), False))
    sent, state, gating = call(
        middle_kernel,
        [(edge, BF16), (wide, BF16), (wide, F32)],
        [tall(prod), tall(edge), (wide, BF16)],
    )(back, state, gating, mask, turned, output_weight, left_weight, right_weight, gate_weight)
    back = exchange(product(exchange(sent), True))
    return call(
        end_kernel,
        [(pair_repr.shape, BF16)],
        [tall(prod), (wide, BF16), (pair_repr.shape, BF16)],
        semaphores=row_count,
        far_out=True,
    )(back, state, gating, turned, output_weight)[0]


def solution(mesh):
    rows = P(AXES, None)
    placed = (P(AXES, None, None), rows) + (P(),) * 10
    return jax.shard_map(
        shards, mesh=mesh, in_specs=placed, out_specs=P(AXES, None, None), check_vma=False
    )
```

time: 66.8 us -> 55.8 us (0.84)
  blocking collectives: 30 us -> 50.9 us
  waiting for transfers between devices: 15.4 us -> 0 us
  local copies, waits for them, and re-layouts: 7.41 us -> 0.02 us
  starting transfers between devices: 5.28 us -> 0 us
  other arithmetic: 4.85 us -> 0 us
  Pallas kernels: 0 us -> 4.63 us
  matrix products: 3.14 us -> 0 us
    all_to_all x2 -> x4, blocking collectives: 30 us -> 50.9 us  [exchange(): lax.all_to_all(rows.reshape(devices, count // devices, columns), AXES, sp...]
    all_to_all x2 -> x0, waiting for transfers between devices: 15.4 us -> none  [to_rows(): lax.all_to_all(shaped, ('grp', 'blk'), split_axis=2, concat_axis=0, tiled...]
    all_to_all x2 -> x0, starting transfers between devices: 5.28 us -> none  [to_rows(): lax.all_to_all(shaped, ('grp', 'blk'), split_axis=2, concat_axis=0, tiled...]
    pallas_call x0 -> x5, Pallas kernels: none -> 4.63 us  [run(): pl.pallas_call(kernel, out_shape=[jax.ShapeDtypeStruct(*s) for s in shape...]
    dot_general x10 -> x0, matrix products: 3.14 us -> none  [the longest x2 1.09 us: shards(): lax.dot_general(normed_out, output_weight[block_index], (((0,), (0,)), ((...]
    unnamed x20 -> x8, local copies, waits for them, and re-layouts: 2.98 us -> 0.02 us
    reduce_sum x8 -> x0, other arithmetic: 2.39 us -> none  [the longest x4 1.55 us: normalize(): average = jnp.mean(values, axis=along, keepdims=True)]
    reshape x2 -> x0, local copies, waits for them, and re-layouts: 1.4 us -> none  [to_rows(): product.reshape(1, per_device, group_count * block_count, row_count, colu...]
  transfers between devices with their start and end apart: 2 -> 0, of which waited for: 2 -> 0; matrix products, arithmetic and copies ran while one was open for 1% -> 0% of each run, Pallas kernels for 0% -> 0%
where the time goes in v2:
time: 55.8 us; the launch traced here: 55.6 us
  blocking collectives  50.9 us (91%)
  Pallas kernels  4.63 us (8%)
    all_to_all x4, blocking collectives, exchange(): lax.all_to_all(rows.reshape(devices, count // devices, columns), AXES, sp...  50.9 us
    pallas_call x5, Pallas kernels, run(): pl.pallas_call(kernel, out_shape=[jax.ShapeDtypeStruct(*s) for s in shape...  4.63 us

profile of v2, /device:TPU:0, one launch (start us, length us, event | category | flops | bytes accessed | tf_op | source)
XLA Modules:
  0.0 55.6 jit_solution(2449295696705533160)
XLA Ops:
  0.0 1.7 %shard_map.118 = (bf16[1024,128]{1,0:T(8,128)(2,1)S(1)}, f32[128,512]{1,0:T(8,128)S(1)}, f32[128,512]{1,0:T(8,128)S(1)}, f32[4,128]{1,0:T(4,128)S(1)}, f32[128,8]{1,0:T(8,128)S(1)}) custom-call(bf16[4,128,128]{2,1,0:T(8,128)(2,1)} %pair_h.1, s32[4,128]{1,0:T(4,128)} %mask_h.1, s32[1,128]{1,0:T(1,128)} %bitcast.17, f32[2,128]{1,0:T(2,128)} %embed_h.1, ...), custom_call_target="tpu_custom_call" | custom-call | tf_op jit(solution)/shard_map/pallas_call | solution.py:217
  1.8 17.7 %all_to_all.20 = bf16[32,32,128]{2,1,0:T(8,128)(2,1)S(1)} all-to-all(bf16[32,32,128]{2,1,0:T(8,128)(2,1)S(1)} %bitcast.16), channel_id=1, replica_groups=mesh['grp'=4,'blk'=8] {'grp','blk'}, dimensions={0} | all-to-all | bytes 524288 | tf_op jit(solution)/shard_map/all_to_all | solution.py:233
  19.5 0.0 copy-start.2
  19.5 0.0 copy-start.3
  19.5 0.5 shard_map.119
  20.0 0.0 copy-start
  20.0 0.0 copy-start.1
  20.0 10.4 %all_to_all.21 = bf16[32,16,128]{2,1,0:T(8,128)(2,1)S(1)} all-to-all(bf16[32,16,128]{2,1,0:T(8,128)(2,1)S(1)} %bitcast.12), channel_id=1, replica_groups=mesh['grp'=4,'blk'=8] {'grp','blk'}, dimensions={0} | all-to-all | bytes 262144 | tf_op jit(solution)/shard_map/all_to_all | solution.py:233
  30.4 0.0 copy-done.2
  30.4 0.0 copy-done.3
  30.4 0.0 copy-done
  30.4 0.0 copy-done.1
  30.4 0.8 %shard_map.120 = (bf16[1024,128]{1,0:T(8,128)(2,1)S(1)}, bf16[128,512]{1,0:T(8,128)(2,1)S(1)}, f32[128,512]{1,0:T(8,128)S(1)}) custom-call(bf16[512,128]{1,0:T(8,128)(2,1)S(1)} %bitcast.11, f32[128,512]{1,0:T(8,128)S(1)} %get-tuple-element.14.state, f32[128,512]{1,0:T(8,128)S(1)} %get-tuple-element.15.gating, f32[4,128]{1,0:T(4,128)S(1)} %get-tuple-element.16.mask, ...), custom_call_target="tpu_custom_call" | custom-call | tf_op jit(solution)/shard_map/pallas_call | solution.py:217
  31.2 12.3 %all_to_all.22 = bf16[32,32,128]{2,1,0:T(8,128)(2,1)S(1)} all-to-all(bf16[32,32,128]{2,1,0:T(8,128)(2,1)S(1)} %bitcast.15), channel_id=1, replica_groups=mesh['grp'=4,'blk'=8] {'grp','blk'}, dimensions={0} | all-to-all | bytes 524288 | tf_op jit(solution)/shard_map/all_to_all | solution.py:233
  43.5 0.5 shard_map.121
  44.0 10.4 %all_to_all.23 = bf16[32,16,128]{2,1,0:T(8,128)(2,1)S(1)} all-to-all(bf16[32,16,128]{2,1,0:T(8,128)(2,1)S(1)} %bitcast.13), channel_id=1, replica_groups=mesh['grp'=4,'blk'=8] {'grp','blk'}, dimensions={0} | all-to-all | bytes 262144 | tf_op jit(solution)/shard_map/all_to_all | solution.py:233
  54.4 1.1 %shard_map.122 = bf16[4,128,128]{2,1,0:T(8,128)(2,1)} custom-call(bf16[512,128]{1,0:T(8,128)(2,1)S(1)} %bitcast.14, bf16[128,512]{1,0:T(8,128)(2,1)S(1)} %get-tuple-element.19.state, f32[128,512]{1,0:T(8,128)S(1)} %get-tuple-element.20.gating, f32[128,8]{1,0:T(8,128)S(1)} %get-tuple-element.17.turned, bf16[2,128,128]{2,1,0:T(8,128)(2,1)S(1)} %copy-done.2), custom_call_target="tpu_custom_call" | custom-call | tf_op jit(solution)/shard_map/pallas_call | solution.py:217
Async XLA Ops:
  19.5 10.9 %copy-start.2 = (bf16[2,128,128]{2,1,0:T(8,128)(2,1)S(1)}, bf16[2,128,128]{2,1,0:T(8,128)(2,1)}, u32[]{:S(2)}) copy-start(bf16[2,128,128]{2,1,0:T(8,128)(2,1)} %weight_o.3) | copy-start | bytes 196612
  19.5 10.9 %copy-start.3 = (bf16[2,128,128]{2,1,0:T(8,128)(2,1)S(1)}, bf16[2,128,128]{2,1,0:T(8,128)(2,1)}, u32[]{:S(2)}) copy-start(bf16[2,128,128]{2,1,0:T(8,128)(2,1)} %gate.1) | copy-start | bytes 196612
  20.0 10.4 %copy-start = (bf16[2,128,256]{2,1,0:T(8,128)(2,1)S(1)}, bf16[2,128,256]{2,1,0:T(8,128)(2,1)}, u32[]{:S(2)}) copy-start(bf16[2,128,256]{2,1,0:T(8,128)(2,1)} %left.1) | copy-start | bytes 393220
  20.0 10.4 %copy-start.1 = (bf16[2,128,256]{2,1,0:T(8,128)(2,1)S(1)}, bf16[2,128,256]{2,1,0:T(8,128)(2,1)}, u32[]{:S(2)}) copy-start(bf16[2,128,256]{2,1,0:T(8,128)(2,1)} %right.1) | copy-start | bytes 393220

commit v3 on v2

v3 whole, which is shorter than its diff:
```python
import functools

import jax
import jax.numpy as jnp
from jax import lax
from jax.experimental import pallas as pl
from jax.experimental.pallas import tpu as pltpu
from jax.sharding import PartitionSpec as P

AXES = ("grp", "blk")
F32, BF16 = jnp.float32, jnp.bfloat16
ON_SUBLANES = (((0,), (0,)), ((), ()))
ON_LANES = (((1,), (1,)), ((), ()))
LANES = 128


def unit(scale):
    down = lax.broadcasted_iota(jnp.int32, (LANES, LANES), 0)
    across = lax.broadcasted_iota(jnp.int32, (LANES, LANES), 1)
    return jnp.where(down == across, scale, 0.0).astype(BF16)


def turn(one, block):
    parts = [
        lax.dot_general(
            one, block[:, at : at + LANES], ON_LANES, preferred_element_type=F32
        ).astype(BF16)
        for at in range(0, block.shape[1], LANES)
    ]
    return jnp.concatenate(parts)


def turn_all(left, right, gate):
    parts = []
    for side in (left, right):
        hidden = side.shape[1] // 2
        parts += [side[:, :hidden] * 0.5, side[:, hidden:]]
    return jnp.transpose(jnp.concatenate(parts + [gate * 0.5], axis=1))


def spread(column):
    return jnp.broadcast_to(column, (column.shape[0], LANES))


def normalize(values, gain, bias):
    average = jnp.mean(values, axis=0, keepdims=True)
    centered = values - average
    variance = jnp.mean(centered * centered, axis=0, keepdims=True)
    return (centered * lax.rsqrt(variance + 1e-05) * gain + bias).astype(BF16)


def put(ref, first, count, stride, values):
    for part in range(ref.shape[0]):
        at = part * LANES
        ref[part, pl.ds(first, count, stride=stride), :] = values[:, at : at + LANES]


def take(ref, first, count, stride):
    rows = pl.ds(first, count, stride=stride)
    return jnp.concatenate([ref[part, rows, :] for part in range(ref.shape[0])], axis=1)


def widen(source, ref):
    for part in range(ref.shape[0]):
        ref[part] = source[:, part * LANES : (part + 1) * LANES].astype(F32)


def pack(ref, out):
    for part in range(ref.shape[0]):
        out[:, part * LANES : (part + 1) * LANES] = ref[part].astype(BF16)


def project(normed, weights, first, mask, e32, gating):
    row_count, columns = mask.shape
    hidden = e32.shape[1] // (2 * row_count)
    projected = jnp.dot(weights, normed, preferred_element_type=F32)
    for at in range(0, normed.shape[1], LANES):
        row, column = divmod(first + at, columns)
        block = projected[:, at : at + LANES]
        kept = mask[row : row + 1, column : column + LANES]
        for side in range(2):
            low = 2 * hidden * side
            values = block[low + hidden : low + 2 * hidden] * kept
            values = (jnp.tanh(block[low : low + hidden]) + 1.0) * values
            rows = pl.ds(side * row_count + row, hidden, stride=2 * row_count)
            e32[column // LANES, rows, :] = values
        gating[:, first + at : first + at + LANES] = jnp.tanh(block[4 * hidden :]) + 1.0


def start_kernel(
    pair_h, mask_h, chain_h, embed_h, gain_h, bias_h, gain_oh, bias_oh, left_h, right_h, gate_h,
    out, state, gating, mask_out, columns_out,
    pair, mask, chain, embed, gain, bias, gain_o, bias_o, left, right, gate,
    e32, rows, arrived,
):
    row_count, columns, channels = pair.shape
    wanted = [
        (pair_h, pair),
        (embed_h, embed),
        (gain_h, gain),
        (bias_h, bias),
        (gain_oh, gain_o),
        (bias_oh, bias_o),
        (chain_h, chain),
        (left_h.at[0], left),
        (right_h.at[0], right),
        (gate_h.at[0], gate),
        (mask_h, mask),
    ]
    moves = [
        pltpu.make_async_copy(source, target, arrived.at[place])
        for place, (source, target) in enumerate(wanted)
    ]
    for move in moves:
        move.start()
    first = lax.axis_index(AXES) * row_count
    one = unit(1.0)
    for move in moves[:7]:
        move.wait()
    rows[0:2, :] = gain_o[...]
    rows[2:4, :] = bias_o[...]
    rows[4:6, :] = gain[...]
    rows[6:8, :] = bias[...]
    turned = jnp.transpose(rows[...])
    columns_out[...] = turned
    gain_c, bias_c = spread(turned[:, 4:5]), spread(turned[:, 6:7])
    rows[0:2, :] = embed[...]
    turned = jnp.transpose(rows[...])
    other, same = spread(turned[:, 0:1]), spread(turned[:, 1:2])
    chains = jnp.broadcast_to(chain[...].astype(F32), (row_count, chain.shape[1]))
    place = lax.broadcasted_iota(jnp.int32, chains.shape, 1)
    mine = first + lax.broadcasted_iota(jnp.int32, chains.shape, 0)
    own = jnp.sum(jnp.where(place == mine, chains, 0.0), axis=1, keepdims=True)
    alike = jnp.where(chains == own, 1.0, 0.0)
    normed = []
    for begin in range(0, row_count * columns, LANES):
        row, column = divmod(begin, columns)
        values = lax.dot_general(
            one, pair[row, column : column + LANES, :], ON_LANES, preferred_element_type=F32
        )
        hit = jnp.broadcast_to(alike[row : row + 1, column : column + LANES], values.shape)
        values = values + jnp.where(hit > 0.5, same, other)
        state[:, begin : begin + LANES] = values
        normed.append(normalize(values, gain_c, bias_c))
    for move in moves[7:]:
        move.wait()
    mask_out[...] = mask[...].astype(F32) * 0.5
    weights = turn_all(left[...], right[...], gate[...])
    for place in range(0, len(normed), 2):
        pair_of = jnp.concatenate(normed[place : place + 2], axis=1)
        project(pair_of, weights, place * LANES, mask_out, e32, gating)
    pack(e32, out)


def apart(low, high, half):
    upper = lax.broadcasted_iota(jnp.int32, low.shape, 1) < half
    firsts = jnp.where(upper, low, pltpu.roll(high, half, 1))
    return firsts, jnp.where(upper, pltpu.roll(low, half, 1), high)


def product_kernel(incoming, devices, x, out):
    columns = x.shape[1]
    row_count = columns // devices
    per_device = x.shape[0] // (2 * columns)
    tiles = x[...].astype(F32).reshape(devices // 2, 2, per_device, 2 * row_count, columns)
    products = []
    for channel in range(per_device):
        sides = apart(tiles[:, 0, channel], tiles[:, 1, channel], row_count)
        left, right = (side.reshape(columns, columns).astype(BF16) for side in sides)
        products.append(
            lax.dot_general(
                left, right, ON_SUBLANES if incoming else ON_LANES, preferred_element_type=F32
            ).reshape(devices // 2, 2 * row_count, columns)
        )
    if per_device == 1:
        out[...] = products[0].reshape(columns, columns).astype(BF16)
        return
    even, odd = [], []
    for channel in range(0, per_device, 2):
        low, high = apart(products[channel], products[channel + 1], row_count)
        even.append(low)
        odd.append(high)
    merged = jnp.stack([jnp.stack(even, axis=1), jnp.stack(odd, axis=1)], axis=1)
    out[...] = merged.reshape(out.shape).astype(BF16)


def finish(y32, first, lanes, columns, gain, bias, weight):
    row_count = y32.shape[1] // gain.shape[0]
    normed = []
    for at in range(first, first + lanes, LANES):
        row, column = divmod(at, columns)
        rows = pl.ds(row, gain.shape[0], stride=row_count)
        normed.append(normalize(y32[column // LANES, rows, :], gain, bias))
    return jnp.dot(weight, jnp.concatenate(normed, axis=1), preferred_element_type=F32)


def middle_kernel(
    y, state, gating, mask, turned, weight_o, left, right, gate,
    out, state_out, gating_out, y32, e32,
):
    row_count, columns = mask.shape
    gain_o, bias_o = spread(turned[:, 0:1]), spread(turned[:, 2:3])
    gain, bias = spread(turned[:, 5:6]), spread(turned[:, 7:8])
    weight = jnp.transpose(weight_o[0] * 0.5)
    weights = turn_all(left[1], right[1], gate[1])
    widen(y, y32)
    for at in range(0, row_count * columns, 2 * LANES):
        lanes = slice(at, at + 2 * LANES)
        update = finish(y32, at, 2 * LANES, columns, gain_o, bias_o, weight)
        stored = (state[:, lanes] + gating[:, lanes] * update).astype(BF16)
        state_out[:, lanes] = stored
        values = stored.astype(F32)
        normed = [normalize(values[:, q : q + LANES], gain, bias) for q in (0, LANES)]
        project(jnp.concatenate(normed, axis=1), weights, at, mask, e32, gating_out)
    pack(e32, out)


def end_kernel(y, state, gating, turned, weight_o, out, y32):
    row_count, columns, channels = out.shape
    one = unit(1.0)
    gain_o, bias_o = spread(turned[:, 1:2]), spread(turned[:, 3:4])
    weight = jnp.transpose(weight_o[1] * 0.5)
    widen(y, y32)
    update = finish(y32, 0, row_count * columns, columns, gain_o, bias_o, weight)
    stored = (state[...].astype(F32) + gating[...] * update).astype(BF16)
    for row in range(row_count):
        lanes = slice(row * columns, (row + 1) * columns)
        out[row] = turn(one, stored[:, lanes])


def call(kernel, shapes, scratch, semaphores=0, far_in=False):
    near = pl.BlockSpec(memory_space=pltpu.VMEM)
    far = pl.BlockSpec(memory_space=pltpu.HBM)

    def run(*operands):
        if far_in:
            operands = [pltpu.with_memory_space_constraint(o, pltpu.HBM) for o in operands]
        return pl.pallas_call(
            kernel,
            out_shape=[jax.ShapeDtypeStruct(*s) for s in shapes],
            in_specs=[far if far_in else near] * len(operands),
            out_specs=[near] * len(shapes),
            scratch_shapes=[pltpu.VMEM(*s) for s in scratch]
            + [pltpu.SemaphoreType.DMA((semaphores,))] * (semaphores > 0),
            compiler_params=pltpu.CompilerParams(vmem_limit_bytes=16 << 20),
        )(*operands)

    return run


def exchange(rows):
    devices = lax.axis_size(AXES[0]) * lax.axis_size(AXES[1])
    count, columns = rows.shape
    moved = lax.all_to_all(
        rows.reshape(devices, count // devices, columns),
        AXES,
        split_axis=0,
        concat_axis=0,
        tiled=True,
    )
    return moved.reshape(count, columns)


def shards(
    pair_repr,
    pair_mask,
    chain_index,
    entity_embed,
    input_gain,
    input_bias,
    left_weight,
    right_weight,
    gate_weight,
    output_gain,
    output_bias,
    output_weight,
):
    row_count, columns, channels = pair_repr.shape
    hidden = output_weight.shape[1]
    devices = lax.axis_size(AXES[0]) * lax.axis_size(AXES[1])
    positions = row_count * columns
    edge = (hidden * 2 * row_count, columns)
    prod = (hidden * row_count, columns)
    wide = (channels, positions)

    def tall(shape):
        return ((shape[1] // LANES, shape[0], LANES), F32)

    columnar = ((channels, 8), F32)
    weights = [left_weight.shape[1:], right_weight.shape[1:], gate_weight.shape[1:]]

    sent, state, gating, mask, turned = call(
        start_kernel,
        [(edge, BF16), (wide, F32), (wide, F32), (pair_mask.shape, F32), columnar],
        [(pair_repr.shape, BF16), (pair_mask.shape, jnp.int32), ((1, columns), jnp.int32)]
        + [((2, channels), F32)] * 5
        + [(shape, BF16) for shape in weights]
        + [tall(edge), ((8, channels), F32)],
        semaphores=11,
        far_in=True,
    )(
        pair_repr, pair_mask, chain_index.reshape(1, -1), entity_embed, input_gain, input_bias,
        output_gain, output_bias, left_weight, right_weight, gate_weight,
    )

    def product(rows, incoming):
        return call(
            functools.partial(product_kernel, incoming, devices),
            [(prod, BF16)],
            [],
        )(rows)[0]

    back = exchange(product(exchange(sent), False))
    sent, state, gating = call(
        middle_kernel,
        [(edge, BF16), (wide, BF16), (wide, F32)],
        [tall(prod), tall(edge)],
    )(back, state, gating, mask, turned, output_weight, left_weight, right_weight, gate_weight)
    back = exchange(product(exchange(sent), True))
    return call(
        end_kernel,
        [(pair_repr.shape, BF16)],
        [tall(prod)],
    )(back, state, gating, turned, output_weight)[0]


def solution(mesh):
    rows = P(AXES, None)
    placed = (P(AXES, None, None), rows) + (P(),) * 10
    return jax.shard_map(
        shards, mesh=mesh, in_specs=placed, out_specs=P(AXES, None, None), check_vma=False
    )
```

time: 55.8 us -> 55.2 us (0.989)
  no operation moved by 1% of the time
where the time goes in v3:
time: 55.2 us; the launch traced here: 55 us
  blocking collectives  50.9 us (92%)
  Pallas kernels  4.1 us (7%)
    all_to_all x4, blocking collectives, exchange(): lax.all_to_all(rows.reshape(devices, count // devices, columns), AXES, sp...  50.9 us
    pallas_call x5, Pallas kernels, run(): pl.pallas_call(kernel, out_shape=[jax.ShapeDtypeStruct(*s) for s in shape...  4.1 us

profile of v3, /device:TPU:0, one launch (start us, length us, event | category | flops | bytes accessed | tf_op | source)
XLA Modules:
  0.0 55.0 jit_solution(13391918370820489103)
XLA Ops:
  0.0 1.8 %shard_map.118 = (bf16[1024,128]{1,0:T(8,128)(2,1)S(1)}, f32[128,512]{1,0:T(8,128)S(1)}, f32[128,512]{1,0:T(8,128)S(1)}, f32[4,128]{1,0:T(4,128)S(1)}, f32[128,8]{1,0:T(8,128)S(1)}) custom-call(bf16[4,128,128]{2,1,0:T(8,128)(2,1)} %pair_h.1, s32[4,128]{1,0:T(4,128)} %mask_h.1, s32[1,128]{1,0:T(1,128)} %bitcast.17, f32[2,128]{1,0:T(2,128)} %embed_h.1, ...), custom_call_target="tpu_custom_call" | custom-call | tf_op jit(solution)/shard_map/pallas_call | solution.py:238
  1.8 17.7 %all_to_all.20 = bf16[32,32,128]{2,1,0:T(8,128)(2,1)S(1)} all-to-all(bf16[32,32,128]{2,1,0:T(8,128)(2,1)S(1)} %bitcast.16), channel_id=1, replica_groups=mesh['grp'=4,'blk'=8] {'grp','blk'}, dimensions={0} | all-to-all | bytes 524288 | tf_op jit(solution)/shard_map/all_to_all | solution.py:254
  19.5 0.0 copy-start.2
  19.5 0.0 copy-start.3
  19.5 0.2 shard_map.119
  19.7 0.0 copy-start
  19.8 0.0 copy-start.1
  19.8 10.4 %all_to_all.21 = bf16[32,16,128]{2,1,0:T(8,128)(2,1)S(1)} all-to-all(bf16[32,16,128]{2,1,0:T(8,128)(2,1)S(1)} %bitcast.12), channel_id=1, replica_groups=mesh['grp'=4,'blk'=8] {'grp','blk'}, dimensions={0} | all-to-all | bytes 262144 | tf_op jit(solution)/shard_map/all_to_all | solution.py:254
  30.2 0.0 copy-done.2
  30.2 0.0 copy-done.3
  30.2 0.0 copy-done
  30.2 0.0 copy-done.1
  30.2 0.7 %shard_map.120 = (bf16[1024,128]{1,0:T(8,128)(2,1)S(1)}, bf16[128,512]{1,0:T(8,128)(2,1)S(1)}, f32[128,512]{1,0:T(8,128)S(1)}) custom-call(bf16[512,128]{1,0:T(8,128)(2,1)S(1)} %bitcast.11, f32[128,512]{1,0:T(8,128)S(1)} %get-tuple-element.14.state, f32[128,512]{1,0:T(8,128)S(1)} %get-tuple-element.15.gating, f32[4,128]{1,0:T(4,128)S(1)} %get-tuple-element.16.mask, ...), custom_call_target="tpu_custom_call" | custom-call | tf_op jit(solution)/shard_map/pallas_call | solution.py:238
  30.9 12.3 %all_to_all.22 = bf16[32,32,128]{2,1,0:T(8,128)(2,1)S(1)} all-to-all(bf16[32,32,128]{2,1,0:T(8,128)(2,1)S(1)} %bitcast.15), channel_id=1, replica_groups=mesh['grp'=4,'blk'=8] {'grp','blk'}, dimensions={0} | all-to-all | bytes 524288 | tf_op jit(solution)/shard_map/all_to_all | solution.py:254
  43.3 0.2 shard_map.121
  43.5 10.4 %all_to_all.23 = bf16[32,16,128]{2,1,0:T(8,128)(2,1)S(1)} all-to-all(bf16[32,16,128]{2,1,0:T(8,128)(2,1)S(1)} %bitcast.13), channel_id=1, replica_groups=mesh['grp'=4,'blk'=8] {'grp','blk'}, dimensions={0} | all-to-all | bytes 262144 | tf_op jit(solution)/shard_map/all_to_all | solution.py:254
  53.9 1.1 %shard_map.122 = bf16[4,128,128]{2,1,0:T(8,128)(2,1)} custom-call(bf16[512,128]{1,0:T(8,128)(2,1)S(1)} %bitcast.14, bf16[128,512]{1,0:T(8,128)(2,1)S(1)} %get-tuple-element.19.state, f32[128,512]{1,0:T(8,128)S(1)} %get-tuple-element.20.gating, f32[128,8]{1,0:T(8,128)S(1)} %get-tuple-element.17.turned, bf16[2,128,128]{2,1,0:T(8,128)(2,1)S(1)} %copy-done.2), custom_call_target="tpu_custom_call" | custom-call | tf_op jit(solution)/shard_map/pallas_call | solution.py:238
Async XLA Ops:
  19.5 10.7 %copy-start.2 = (bf16[2,128,128]{2,1,0:T(8,128)(2,1)S(1)}, bf16[2,128,128]{2,1,0:T(8,128)(2,1)}, u32[]{:S(2)}) copy-start(bf16[2,128,128]{2,1,0:T(8,128)(2,1)} %weight_o.3) | copy-start | bytes 196612
  19.5 10.7 %copy-start.3 = (bf16[2,128,128]{2,1,0:T(8,128)(2,1)S(1)}, bf16[2,128,128]{2,1,0:T(8,128)(2,1)}, u32[]{:S(2)}) copy-start(bf16[2,128,128]{2,1,0:T(8,128)(2,1)} %gate.1) | copy-start | bytes 196612
  19.7 10.4 %copy-start = (bf16[2,128,256]{2,1,0:T(8,128)(2,1)S(1)}, bf16[2,128,256]{2,1,0:T(8,128)(2,1)}, u32[]{:S(2)}) copy-start(bf16[2,128,256]{2,1,0:T(8,128)(2,1)} %left.1) | copy-start | bytes 393220
  19.8 10.4 %copy-start.1 = (bf16[2,128,256]{2,1,0:T(8,128)(2,1)S(1)}, bf16[2,128,256]{2,1,0:T(8,128)(2,1)}, u32[]{:S(2)}) copy-start(bf16[2,128,256]{2,1,0:T(8,128)(2,1)} %right.1) | copy-start | bytes 393220

commit v4 on v3

--- a/solution.py
+++ b/solution.py
@@ -30,12 +30,16 @@
     return jnp.concatenate(parts)
 
 
-def turn_all(left, right, gate):
-    parts = []
-    for side in (left, right):
-        hidden = side.shape[1] // 2
-        parts += [side[:, :hidden] * 0.5, side[:, hidden:]]
-    return jnp.transpose(jnp.concatenate(parts + [gate * 0.5], axis=1))
+def turn_all(parts):
+    scaled = [part if place in (1, 3) else part * 0.5 for place, part in enumerate(parts)]
+    return jnp.transpose(jnp.concatenate(scaled, axis=1))
+
+
+def halves(left, right, gate):
+    hidden = left.shape[-1] // 2
+    return [
+        left[..., :hidden], left[..., hidden:], right[..., :hidden], right[..., hidden:], gate
+    ]
 
 
 def spread(column):
@@ -90,41 +94,35 @@
 def start_kernel(
     pair_h, mask_h, chain_h, embed_h, gain_h, bias_h, gain_oh, bias_oh, left_h, right_h, gate_h,
     out, state, gating, mask_out, columns_out,
-    pair, mask, chain, embed, gain, bias, gain_o, bias_o, left, right, gate,
-    e32, rows, arrived,
+    pair, mask, chain, small, weights, e32, rows, arrived,
 ):
     row_count, columns, channels = pair.shape
-    wanted = [
-        (pair_h, pair),
-        (embed_h, embed),
-        (gain_h, gain),
-        (bias_h, bias),
-        (gain_oh, gain_o),
-        (bias_oh, bias_o),
-        (chain_h, chain),
-        (left_h.at[0], left),
-        (right_h.at[0], right),
-        (gate_h.at[0], gate),
-        (mask_h, mask),
-    ]
-    moves = [
-        pltpu.make_async_copy(source, target, arrived.at[place])
-        for place, (source, target) in enumerate(wanted)
-    ]
-    for move in moves:
-        move.start()
+    moves = [(pair_h, pair, 0)]
+    smalls = (embed_h, gain_h, bias_h, gain_oh, bias_oh)
+    moves += [(source, small.at[place], 1) for place, source in enumerate(smalls)]
+    moves += [(chain_h, chain, 2)]
+    hidden = weights.shape[2]
+    for place, source in enumerate((left_h, left_h, right_h, right_h, gate_h)):
+        lanes = pl.ds(place % 2 * hidden, hidden)
+        moves += [(source.at[0, :, lanes], weights.at[place], 3)]
+    moves += [(mask_h, mask, 4)]
+    for source, target, which in moves:
+        pltpu.make_async_copy(source, target, arrived.at[which]).start()
     first = lax.axis_index(AXES) * row_count
     one = unit(1.0)
-    for move in moves[:7]:
-        move.wait()
-    rows[0:2, :] = gain_o[...]
-    rows[2:4, :] = bias_o[...]
-    rows[4:6, :] = gain[...]
-    rows[6:8, :] = bias[...]
+
+    def wait(whole, which):
+        pltpu.make_async_copy(whole, whole, arrived.at[which]).wait()
+
+    wait(small, 1)
+    wait(chain, 2)
+    wait(pair, 0)
+    for place in range(4):
+        rows[2 * place : 2 * place + 2, :] = small[(3, 4, 1, 2)[place]]
     turned = jnp.transpose(rows[...])
     columns_out[...] = turned
     gain_c, bias_c = spread(turned[:, 4:5]), spread(turned[:, 6:7])
-    rows[0:2, :] = embed[...]
+    rows[0:2, :] = small[0]
     turned = jnp.transpose(rows[...])
     other, same = spread(turned[:, 0:1]), spread(turned[:, 1:2])
     chains = jnp.broadcast_to(chain[...].astype(F32), (row_count, chain.shape[1]))
@@ -142,13 +140,13 @@
         values = values + jnp.where(hit > 0.5, same, other)
         state[:, begin : begin + LANES] = values
         normed.append(normalize(values, gain_c, bias_c))
-    for move in moves[7:]:
-        move.wait()
+    wait(weights, 3)
+    wait(mask, 4)
     mask_out[...] = mask[...].astype(F32) * 0.5
-    weights = turn_all(left[...], right[...], gate[...])
+    turned = turn_all([weights[place] for place in range(weights.shape[0])])
     for place in range(0, len(normed), 2):
         pair_of = jnp.concatenate(normed[place : place + 2], axis=1)
-        project(pair_of, weights, place * LANES, mask_out, e32, gating)
+        project(pair_of, turned, place * LANES, mask_out, e32, gating)
     pack(e32, out)
 
 
@@ -202,7 +200,7 @@
     gain_o, bias_o = spread(turned[:, 0:1]), spread(turned[:, 2:3])
     gain, bias = spread(turned[:, 5:6]), spread(turned[:, 7:8])
     weight = jnp.transpose(weight_o[0] * 0.5)
-    weights = turn_all(left[1], right[1], gate[1])
+    weights = turn_all(halves(left[1], right[1], gate[1]))
     widen(y, y32)
     for at in range(0, row_count * columns, 2 * LANES):
         lanes = slice(at, at + 2 * LANES)
@@ -287,16 +285,13 @@
         return ((shape[1] // LANES, shape[0], LANES), F32)
 
     columnar = ((channels, 8), F32)
-    weights = [left_weight.shape[1:], right_weight.shape[1:], gate_weight.shape[1:]]
 
     sent, state, gating, mask, turned = call(
         start_kernel,
         [(edge, BF16), (wide, F32), (wide, F32), (pair_mask.shape, F32), columnar],
         [(pair_repr.shape, BF16), (pair_mask.shape, jnp.int32), ((1, columns), jnp.int32)]
-        + [((2, channels), F32)] * 5
-        + [(shape, BF16) for shape in weights]
-        + [tall(edge), ((8, channels), F32)],
-        semaphores=11,
+        + [((5, 2, channels), F32), ((5, channels, hidden), BF16), tall(edge), ((8, channels), F32)],
+        semaphores=5,
         far_in=True,
     )(
         pair_repr, pair_mask, chain_index.reshape(1, -1), entity_embed, input_gain, input_bias,

time: 55.2 us -> 55.2 us (level)
  no operation moved by 1% of the time
where the time goes in v4:
time: 55.2 us; the launch traced here: 55 us
  blocking collectives  50.9 us (92%)
  Pallas kernels  4.03 us (7%)
    all_to_all x4, blocking collectives, exchange(): lax.all_to_all(rows.reshape(devices, count // devices, columns), AXES, sp...  50.9 us
    pallas_call x5, Pallas kernels, run(): pl.pallas_call(kernel, out_shape=[jax.ShapeDtypeStruct(*s) for s in shape...  4.03 us

profile of v4, /device:TPU:0, one launch (start us, length us, event | category | flops | bytes accessed | tf_op | source)
XLA Modules:
  0.0 55.0 jit_solution(2772583253070066511)
XLA Ops:
  0.0 1.7 %shard_map.118 = (bf16[1024,128]{1,0:T(8,128)(2,1)S(1)}, f32[128,512]{1,0:T(8,128)S(1)}, f32[128,512]{1,0:T(8,128)S(1)}, f32[4,128]{1,0:T(4,128)S(1)}, f32[128,8]{1,0:T(8,128)S(1)}) custom-call(bf16[4,128,128]{2,1,0:T(8,128)(2,1)} %pair_h.1, s32[4,128]{1,0:T(4,128)} %mask_h.1, s32[1,128]{1,0:T(1,128)} %bitcast.17, f32[2,128]{1,0:T(2,128)} %embed_h.1, ...), custom_call_target="tpu_custom_call" | custom-call | tf_op jit(solution)/shard_map/pallas_call | solution.py:236
  1.7 17.7 %all_to_all.20 = bf16[32,32,128]{2,1,0:T(8,128)(2,1)S(1)} all-to-all(bf16[32,32,128]{2,1,0:T(8,128)(2,1)S(1)} %bitcast.16), channel_id=1, replica_groups=mesh['grp'=4,'blk'=8] {'grp','blk'}, dimensions={0} | all-to-all | bytes 524288 | tf_op jit(solution)/shard_map/all_to_all | solution.py:252
  19.5 0.0 copy-start.2
  19.5 0.0 copy-start.3
  19.5 0.2 shard_map.119
  19.7 0.0 copy-start
  19.7 0.0 copy-start.1
  19.7 10.4 %all_to_all.21 = bf16[32,16,128]{2,1,0:T(8,128)(2,1)S(1)} all-to-all(bf16[32,16,128]{2,1,0:T(8,128)(2,1)S(1)} %bitcast.12), channel_id=1, replica_groups=mesh['grp'=4,'blk'=8] {'grp','blk'}, dimensions={0} | all-to-all | bytes 262144 | tf_op jit(solution)/shard_map/all_to_all | solution.py:252
  30.1 0.0 copy-done.2
  30.1 0.0 copy-done.3
  30.1 0.0 copy-done
  30.1 0.0 copy-done.1
  30.1 0.7 %shard_map.120 = (bf16[1024,128]{1,0:T(8,128)(2,1)S(1)}, bf16[128,512]{1,0:T(8,128)(2,1)S(1)}, f32[128,512]{1,0:T(8,128)S(1)}) custom-call(bf16[512,128]{1,0:T(8,128)(2,1)S(1)} %bitcast.11, f32[128,512]{1,0:T(8,128)S(1)} %get-tuple-element.14.state, f32[128,512]{1,0:T(8,128)S(1)} %get-tuple-element.15.gating, f32[4,128]{1,0:T(4,128)S(1)} %get-tuple-element.16.mask, ...), custom_call_target="tpu_custom_call" | custom-call | tf_op jit(solution)/shard_map/pallas_call | solution.py:236
  30.9 12.3 %all_to_all.22 = bf16[32,32,128]{2,1,0:T(8,128)(2,1)S(1)} all-to-all(bf16[32,32,128]{2,1,0:T(8,128)(2,1)S(1)} %bitcast.15), channel_id=1, replica_groups=mesh['grp'=4,'blk'=8] {'grp','blk'}, dimensions={0} | all-to-all | bytes 524288 | tf_op jit(solution)/shard_map/all_to_all | solution.py:252
  43.2 0.2 shard_map.121
  43.5 10.4 %all_to_all.23 = bf16[32,16,128]{2,1,0:T(8,128)(2,1)S(1)} all-to-all(bf16[32,16,128]{2,1,0:T(8,128)(2,1)S(1)} %bitcast.13), channel_id=1, replica_groups=mesh['grp'=4,'blk'=8] {'grp','blk'}, dimensions={0} | all-to-all | bytes 262144 | tf_op jit(solution)/shard_map/all_to_all | solution.py:252
  53.9 1.1 %shard_map.122 = bf16[4,128,128]{2,1,0:T(8,128)(2,1)} custom-call(bf16[512,128]{1,0:T(8,128)(2,1)S(1)} %bitcast.14, bf16[128,512]{1,0:T(8,128)(2,1)S(1)} %get-tuple-element.19.state, f32[128,512]{1,0:T(8,128)S(1)} %get-tuple-element.20.gating, f32[128,8]{1,0:T(8,128)S(1)} %get-tuple-element.17.turned, bf16[2,128,128]{2,1,0:T(8,128)(2,1)S(1)} %copy-done.2), custom_call_target="tpu_custom_call" | custom-call | tf_op jit(solution)/shard_map/pallas_call | solution.py:236
Async XLA Ops:
  19.5 10.7 %copy-start.2 = (bf16[2,128,128]{2,1,0:T(8,128)(2,1)S(1)}, bf16[2,128,128]{2,1,0:T(8,128)(2,1)}, u32[]{:S(2)}) copy-start(bf16[2,128,128]{2,1,0:T(8,128)(2,1)} %weight_o.3) | copy-start | bytes 196612
  19.5 10.7 %copy-start.3 = (bf16[2,128,128]{2,1,0:T(8,128)(2,1)S(1)}, bf16[2,128,128]{2,1,0:T(8,128)(2,1)}, u32[]{:S(2)}) copy-start(bf16[2,128,128]{2,1,0:T(8,128)(2,1)} %gate.1) | copy-start | bytes 196612
  19.7 10.4 %copy-start = (bf16[2,128,256]{2,1,0:T(8,128)(2,1)S(1)}, bf16[2,128,256]{2,1,0:T(8,128)(2,1)}, u32[]{:S(2)}) copy-start(bf16[2,128,256]{2,1,0:T(8,128)(2,1)} %left.1) | copy-start | bytes 393220
  19.7 10.4 %copy-start.1 = (bf16[2,128,256]{2,1,0:T(8,128)(2,1)S(1)}, bf16[2,128,256]{2,1,0:T(8,128)(2,1)}, u32[]{:S(2)}) copy-start(bf16[2,128,256]{2,1,0:T(8,128)(2,1)} %right.1) | copy-start | bytes 393220

commit v5 on v4

--- a/solution.py
+++ b/solution.py
@@ -97,7 +97,7 @@
     pair, mask, chain, small, weights, e32, rows, arrived,
 ):
     row_count, columns, channels = pair.shape
-    moves = [(pair_h, pair, 0)]
+    moves = [(pair_h.at[row], pair.at[row], 0) for row in range(row_count)]
     smalls = (embed_h, gain_h, bias_h, gain_oh, bias_oh)
     moves += [(source, small.at[place], 1) for place, source in enumerate(smalls)]
     moves += [(chain_h, chain, 2)]

time: 55.2 us -> 55.1 us (level)
  no operation moved by 1% of the time
where the time goes in v5:
time: 55.1 us; the launch traced here: 54.9 us
  blocking collectives  50.9 us (92%)
  Pallas kernels  3.94 us (7%)
    all_to_all x4, blocking collectives, exchange(): lax.all_to_all(rows.reshape(devices, count // devices, columns), AXES, sp...  50.9 us
    pallas_call x5, Pallas kernels, run(): pl.pallas_call(kernel, out_shape=[jax.ShapeDtypeStruct(*s) for s in shape...  3.94 us

profile of v5, /device:TPU:0, one launch (start us, length us, event | category | flops | bytes accessed | tf_op | source)
XLA Modules:
  0.0 54.9 jit_solution(7335569740980271969)
XLA Ops:
  0.0 1.6 %shard_map.118 = (bf16[1024,128]{1,0:T(8,128)(2,1)S(1)}, f32[128,512]{1,0:T(8,128)S(1)}, f32[128,512]{1,0:T(8,128)S(1)}, f32[4,128]{1,0:T(4,128)S(1)}, f32[128,8]{1,0:T(8,128)S(1)}) custom-call(bf16[4,128,128]{2,1,0:T(8,128)(2,1)} %pair_h.1, s32[4,128]{1,0:T(4,128)} %mask_h.1, s32[1,128]{1,0:T(1,128)} %bitcast.17, f32[2,128]{1,0:T(2,128)} %embed_h.1, ...), custom_call_target="tpu_custom_call" | custom-call | tf_op jit(solution)/shard_map/pallas_call | solution.py:236
  1.6 17.7 %all_to_all.20 = bf16[32,32,128]{2,1,0:T(8,128)(2,1)S(1)} all-to-all(bf16[32,32,128]{2,1,0:T(8,128)(2,1)S(1)} %bitcast.16), channel_id=1, replica_groups=mesh['grp'=4,'blk'=8] {'grp','blk'}, dimensions={0} | all-to-all | bytes 524288 | tf_op jit(solution)/shard_map/all_to_all | solution.py:252
  19.4 0.0 copy-start.2
  19.4 0.0 copy-start.3
  19.4 0.2 shard_map.119
  19.6 0.0 copy-start
  19.6 0.0 copy-start.1
  19.6 10.4 %all_to_all.21 = bf16[32,16,128]{2,1,0:T(8,128)(2,1)S(1)} all-to-all(bf16[32,16,128]{2,1,0:T(8,128)(2,1)S(1)} %bitcast.12), channel_id=1, replica_groups=mesh['grp'=4,'blk'=8] {'grp','blk'}, dimensions={0} | all-to-all | bytes 262144 | tf_op jit(solution)/shard_map/all_to_all | solution.py:252
  30.0 0.0 copy-done.2
  30.0 0.0 copy-done.3
  30.0 0.0 copy-done
  30.0 0.0 copy-done.1
  30.0 0.7 %shard_map.120 = (bf16[1024,128]{1,0:T(8,128)(2,1)S(1)}, bf16[128,512]{1,0:T(8,128)(2,1)S(1)}, f32[128,512]{1,0:T(8,128)S(1)}) custom-call(bf16[512,128]{1,0:T(8,128)(2,1)S(1)} %bitcast.11, f32[128,512]{1,0:T(8,128)S(1)} %get-tuple-element.14.state, f32[128,512]{1,0:T(8,128)S(1)} %get-tuple-element.15.gating, f32[4,128]{1,0:T(4,128)S(1)} %get-tuple-element.16.mask, ...), custom_call_target="tpu_custom_call" | custom-call | tf_op jit(solution)/shard_map/pallas_call | solution.py:236
  30.8 12.3 %all_to_all.22 = bf16[32,32,128]{2,1,0:T(8,128)(2,1)S(1)} all-to-all(bf16[32,32,128]{2,1,0:T(8,128)(2,1)S(1)} %bitcast.15), channel_id=1, replica_groups=mesh['grp'=4,'blk'=8] {'grp','blk'}, dimensions={0} | all-to-all | bytes 524288 | tf_op jit(solution)/shard_map/all_to_all | solution.py:252
  43.1 0.2 shard_map.121
  43.4 10.4 %all_to_all.23 = bf16[32,16,128]{2,1,0:T(8,128)(2,1)S(1)} all-to-all(bf16[32,16,128]{2,1,0:T(8,128)(2,1)S(1)} %bitcast.13), channel_id=1, replica_groups=mesh['grp'=4,'blk'=8] {'grp','blk'}, dimensions={0} | all-to-all | bytes 262144 | tf_op jit(solution)/shard_map/all_to_all | solution.py:252
  53.8 1.1 %shard_map.122 = bf16[4,128,128]{2,1,0:T(8,128)(2,1)} custom-call(bf16[512,128]{1,0:T(8,128)(2,1)S(1)} %bitcast.14, bf16[128,512]{1,0:T(8,128)(2,1)S(1)} %get-tuple-element.19.state, f32[128,512]{1,0:T(8,128)S(1)} %get-tuple-element.20.gating, f32[128,8]{1,0:T(8,128)S(1)} %get-tuple-element.17.turned, bf16[2,128,128]{2,1,0:T(8,128)(2,1)S(1)} %copy-done.2), custom_call_target="tpu_custom_call" | custom-call | tf_op jit(solution)/shard_map/pallas_call | solution.py:236
Async XLA Ops:
  19.4 10.7 %copy-start.2 = (bf16[2,128,128]{2,1,0:T(8,128)(2,1)S(1)}, bf16[2,128,128]{2,1,0:T(8,128)(2,1)}, u32[]{:S(2)}) copy-start(bf16[2,128,128]{2,1,0:T(8,128)(2,1)} %weight_o.3) | copy-start | bytes 196612
  19.4 10.7 %copy-start.3 = (bf16[2,128,128]{2,1,0:T(8,128)(2,1)S(1)}, bf16[2,128,128]{2,1,0:T(8,128)(2,1)}, u32[]{:S(2)}) copy-start(bf16[2,128,128]{2,1,0:T(8,128)(2,1)} %gate.1) | copy-start | bytes 196612
  19.6 10.4 %copy-start = (bf16[2,128,256]{2,1,0:T(8,128)(2,1)S(1)}, bf16[2,128,256]{2,1,0:T(8,128)(2,1)}, u32[]{:S(2)}) copy-start(bf16[2,128,256]{2,1,0:T(8,128)(2,1)} %left.1) | copy-start | bytes 393220
  19.6 10.4 %copy-start.1 = (bf16[2,128,256]{2,1,0:T(8,128)(2,1)S(1)}, bf16[2,128,256]{2,1,0:T(8,128)(2,1)}, u32[]{:S(2)}) copy-start(bf16[2,128,256]{2,1,0:T(8,128)(2,1)} %right.1) | copy-start | bytes 393220

commit v6 on v5

--- a/solution.py
+++ b/solution.py
@@ -215,7 +215,6 @@
 
 def end_kernel(y, state, gating, turned, weight_o, out, y32):
     row_count, columns, channels = out.shape
-    one = unit(1.0)
     gain_o, bias_o = spread(turned[:, 1:2]), spread(turned[:, 3:4])
     weight = jnp.transpose(weight_o[1] * 0.5)
     widen(y, y32)
@@ -223,7 +222,7 @@
     stored = (state[...].astype(F32) + gating[...] * update).astype(BF16)
     for row in range(row_count):
         lanes = slice(row * columns, (row + 1) * columns)
-        out[row] = turn(one, stored[:, lanes])
+        out[row] = jnp.transpose(stored[:, lanes])
 
 
 def call(kernel, shapes, scratch, semaphores=0, far_in=False):

time: 55.1 us -> 55.1 us (level)
  no operation moved by 1% of the time
where the time goes in v6:
time: 55.1 us; the launch traced here: 54.8 us
  blocking collectives  50.9 us (92%)
  Pallas kernels  3.85 us (7%)
    all_to_all x4, blocking collectives, exchange(): lax.all_to_all(rows.reshape(devices, count // devices, columns), AXES, sp...  50.9 us
    pallas_call x5, Pallas kernels, run(): pl.pallas_call(kernel, out_shape=[jax.ShapeDtypeStruct(*s) for s in shape...  3.85 us

profile of v6, /device:TPU:0, one launch (start us, length us, event | category | flops | bytes accessed | tf_op | source)
XLA Modules:
  0.0 54.8 jit_solution(17407791229578063216)
XLA Ops:
  0.0 1.6 %shard_map.118 = (bf16[1024,128]{1,0:T(8,128)(2,1)S(1)}, f32[128,512]{1,0:T(8,128)S(1)}, f32[128,512]{1,0:T(8,128)S(1)}, f32[4,128]{1,0:T(4,128)S(1)}, f32[128,8]{1,0:T(8,128)S(1)}) custom-call(bf16[4,128,128]{2,1,0:T(8,128)(2,1)} %pair_h.1, s32[4,128]{1,0:T(4,128)} %mask_h.1, s32[1,128]{1,0:T(1,128)} %bitcast.17, f32[2,128]{1,0:T(2,128)} %embed_h.1, ...), custom_call_target="tpu_custom_call" | custom-call | tf_op jit(solution)/shard_map/pallas_call | solution.py:235
  1.6 17.7 %all_to_all.20 = bf16[32,32,128]{2,1,0:T(8,128)(2,1)S(1)} all-to-all(bf16[32,32,128]{2,1,0:T(8,128)(2,1)S(1)} %bitcast.16), channel_id=1, replica_groups=mesh['grp'=4,'blk'=8] {'grp','blk'}, dimensions={0} | all-to-all | bytes 524288 | tf_op jit(solution)/shard_map/all_to_all | solution.py:251
  19.4 0.0 copy-start.2
  19.4 0.0 copy-start.3
  19.4 0.2 shard_map.119
  19.6 0.0 copy-start
  19.6 0.0 copy-start.1
  19.6 10.4 %all_to_all.21 = bf16[32,16,128]{2,1,0:T(8,128)(2,1)S(1)} all-to-all(bf16[32,16,128]{2,1,0:T(8,128)(2,1)S(1)} %bitcast.12), channel_id=1, replica_groups=mesh['grp'=4,'blk'=8] {'grp','blk'}, dimensions={0} | all-to-all | bytes 262144 | tf_op jit(solution)/shard_map/all_to_all | solution.py:251
  30.0 0.0 copy-done.2
  30.0 0.0 copy-done.3
  30.0 0.0 copy-done
  30.0 0.0 copy-done.1
  30.0 0.7 %shard_map.120 = (bf16[1024,128]{1,0:T(8,128)(2,1)S(1)}, bf16[128,512]{1,0:T(8,128)(2,1)S(1)}, f32[128,512]{1,0:T(8,128)S(1)}) custom-call(bf16[512,128]{1,0:T(8,128)(2,1)S(1)} %bitcast.11, f32[128,512]{1,0:T(8,128)S(1)} %get-tuple-element.14.state, f32[128,512]{1,0:T(8,128)S(1)} %get-tuple-element.15.gating, f32[4,128]{1,0:T(4,128)S(1)} %get-tuple-element.16.mask, ...), custom_call_target="tpu_custom_call" | custom-call | tf_op jit(solution)/shard_map/pallas_call | solution.py:235
  30.8 12.3 %all_to_all.22 = bf16[32,32,128]{2,1,0:T(8,128)(2,1)S(1)} all-to-all(bf16[32,32,128]{2,1,0:T(8,128)(2,1)S(1)} %bitcast.15), channel_id=1, replica_groups=mesh['grp'=4,'blk'=8] {'grp','blk'}, dimensions={0} | all-to-all | bytes 524288 | tf_op jit(solution)/shard_map/all_to_all | solution.py:251
  43.1 0.2 shard_map.121
  43.4 10.4 %all_to_all.23 = bf16[32,16,128]{2,1,0:T(8,128)(2,1)S(1)} all-to-all(bf16[32,16,128]{2,1,0:T(8,128)(2,1)S(1)} %bitcast.13), channel_id=1, replica_groups=mesh['grp'=4,'blk'=8] {'grp','blk'}, dimensions={0} | all-to-all | bytes 262144 | tf_op jit(solution)/shard_map/all_to_all | solution.py:251
  53.8 1.0 %shard_map.122 = bf16[4,128,128]{2,1,0:T(8,128)(2,1)} custom-call(bf16[512,128]{1,0:T(8,128)(2,1)S(1)} %bitcast.14, bf16[128,512]{1,0:T(8,128)(2,1)S(1)} %get-tuple-element.19.state, f32[128,512]{1,0:T(8,128)S(1)} %get-tuple-element.20.gating, f32[128,8]{1,0:T(8,128)S(1)} %get-tuple-element.17.turned, bf16[2,128,128]{2,1,0:T(8,128)(2,1)S(1)} %copy-done.2), custom_call_target="tpu_custom_call" | custom-call | tf_op jit(solution)/shard_map/pallas_call | solution.py:235
Async XLA Ops:
  19.4 10.7 %copy-start.2 = (bf16[2,128,128]{2,1,0:T(8,128)(2,1)S(1)}, bf16[2,128,128]{2,1,0:T(8,128)(2,1)}, u32[]{:S(2)}) copy-start(bf16[2,128,128]{2,1,0:T(8,128)(2,1)} %weight_o.3) | copy-start | bytes 196612
  19.4 10.7 %copy-start.3 = (bf16[2,128,128]{2,1,0:T(8,128)(2,1)S(1)}, bf16[2,128,128]{2,1,0:T(8,128)(2,1)}, u32[]{:S(2)}) copy-start(bf16[2,128,128]{2,1,0:T(8,128)(2,1)} %gate.1) | copy-start | bytes 196612
  19.6 10.4 %copy-start = (bf16[2,128,256]{2,1,0:T(8,128)(2,1)S(1)}, bf16[2,128,256]{2,1,0:T(8,128)(2,1)}, u32[]{:S(2)}) copy-start(bf16[2,128,256]{2,1,0:T(8,128)(2,1)} %left.1) | copy-start | bytes 393220
  19.6 10.4 %copy-start.1 = (bf16[2,128,256]{2,1,0:T(8,128)(2,1)S(1)}, bf16[2,128,256]{2,1,0:T(8,128)(2,1)}, u32[]{:S(2)}) copy-start(bf16[2,128,256]{2,1,0:T(8,128)(2,1)} %right.1) | copy-start | bytes 393220

commit v7 on v6

--- a/solution.py
+++ b/solution.py
@@ -156,15 +156,18 @@
     return firsts, jnp.where(upper, pltpu.roll(low, half, 1), high)
 
 
-def product_kernel(incoming, devices, x, out):
+def product_kernel(incoming, row_count, x, out):
     columns = x.shape[1]
-    row_count = columns // devices
-    per_device = x.shape[0] // (2 * columns)
-    tiles = x[...].astype(F32).reshape(devices // 2, 2, per_device, 2 * row_count, columns)
+    devices = columns // row_count
+    per_device = out.shape[0] // columns
+    sources = x.shape[0] // (per_device * 2 * row_count)
+    tiles = x[...].astype(F32).reshape(sources // 2, 2, per_device, 2 * row_count, columns)
     products = []
     for channel in range(per_device):
         sides = apart(tiles[:, 0, channel], tiles[:, 1, channel], row_count)
-        left, right = (side.reshape(columns, columns).astype(BF16) for side in sides)
+        left, right = (
+            side.reshape(sources * row_count, columns).astype(BF16) for side in sides
+        )
         products.append(
             lax.dot_general(
                 left, right, ON_SUBLANES if incoming else ON_LANES, preferred_element_type=F32
@@ -217,7 +220,10 @@
     row_count, columns, channels = out.shape
     gain_o, bias_o = spread(turned[:, 1:2]), spread(turned[:, 3:4])
     weight = jnp.transpose(weight_o[1] * 0.5)
-    widen(y, y32)
+    half = y.shape[0] // 2
+    for part in range(y32.shape[0]):
+        lanes = slice(part * LANES, (part + 1) * LANES)
+        y32[part] = y[:half, lanes].astype(F32) + y[half:, lanes].astype(F32)
     update = finish(y32, 0, row_count * columns, columns, gain_o, bias_o, weight)
     stored = (state[...].astype(F32) + gating[...] * update).astype(BF16)
     for row in range(row_count):
@@ -245,15 +251,20 @@
     return run
 
 
-def exchange(rows):
+def exchange(rows, halves=1):
     devices = lax.axis_size(AXES[0]) * lax.axis_size(AXES[1])
+    part = devices // halves
+    groups = None
+    if halves > 1:
+        groups = [list(range(at, at + part)) for at in range(0, devices, part)]
     count, columns = rows.shape
     moved = lax.all_to_all(
-        rows.reshape(devices, count // devices, columns),
+        rows.reshape(part, count // part, columns),
         AXES,
         split_axis=0,
         concat_axis=0,
         tiled=True,
+        axis_index_groups=groups,
     )
     return moved.reshape(count, columns)
 
@@ -297,20 +308,20 @@
         output_gain, output_bias, left_weight, right_weight, gate_weight,
     )
 
-    def product(rows, incoming):
+    def product(rows, incoming, halves):
         return call(
-            functools.partial(product_kernel, incoming, devices),
-            [(prod, BF16)],
+            functools.partial(product_kernel, incoming, row_count),
+            [((prod[0] * halves, columns), BF16)],
             [],
         )(rows)[0]
 
-    back = exchange(product(exchange(sent), False))
+    back = exchange(product(exchange(sent), False, 1))
     sent, state, gating = call(
         middle_kernel,
         [(edge, BF16), (wide, BF16), (wide, F32)],
         [tall(prod), tall(edge)],
     )(back, state, gating, mask, turned, output_weight, left_weight, right_weight, gate_weight)
-    back = exchange(product(exchange(sent), True))
+    back = exchange(product(exchange(sent, 2), True, 2))
     return call(
         end_kernel,
         [(pair_repr.shape, BF16)],

time: 55.1 us -> 55 us (level)
  no operation moved by 1% of the time
where the time goes in v7:
time: 55 us; the launch traced here: 54.7 us
  blocking collectives  50.7 us (92%)
  Pallas kernels  3.91 us (7%)
    all_to_all x4, blocking collectives, exchange(): lax.all_to_all(rows.reshape(part, count // part, columns), AXES, split_ax...  50.7 us
    pallas_call x5, Pallas kernels, run(): pl.pallas_call(kernel, out_shape=[jax.ShapeDtypeStruct(*s) for s in shape...  3.91 us

profile of v7, /device:TPU:0, one launch (start us, length us, event | category | flops | bytes accessed | tf_op | source)
XLA Modules:
  0.0 54.7 jit_solution(11697848596954892657)
XLA Ops:
  0.0 1.6 %shard_map.118 = (bf16[1024,128]{1,0:T(8,128)(2,1)S(1)}, f32[128,512]{1,0:T(8,128)S(1)}, f32[128,512]{1,0:T(8,128)S(1)}, f32[4,128]{1,0:T(4,128)S(1)}, f32[128,8]{1,0:T(8,128)S(1)}) custom-call(bf16[4,128,128]{2,1,0:T(8,128)(2,1)} %pair_h.1, s32[4,128]{1,0:T(4,128)} %mask_h.1, s32[1,128]{1,0:T(1,128)} %bitcast.17, f32[2,128]{1,0:T(2,128)} %embed_h.1, ...), custom_call_target="tpu_custom_call" | custom-call | tf_op jit(solution)/shard_map/pallas_call | solution.py:241
  1.6 17.7 %all_to_all.20 = bf16[32,32,128]{2,1,0:T(8,128)(2,1)S(1)} all-to-all(bf16[32,32,128]{2,1,0:T(8,128)(2,1)S(1)} %bitcast.16), channel_id=1, replica_groups=mesh['grp'=4,'blk'=8] {'grp','blk'}, dimensions={0} | all-to-all | bytes 524288 | tf_op jit(solution)/shard_map/all_to_all | solution.py:261
  19.4 0.0 copy-start.2
  19.4 0.0 copy-start.3
  19.4 0.2 shard_map.119
  19.6 0.0 copy-start
  19.6 0.0 copy-start.1
  19.6 10.4 %all_to_all.21 = bf16[32,16,128]{2,1,0:T(8,128)(2,1)S(1)} all-to-all(bf16[32,16,128]{2,1,0:T(8,128)(2,1)S(1)} %bitcast.14), channel_id=1, replica_groups=mesh['grp'=4,'blk'=8] {'grp','blk'}, dimensions={0} | all-to-all | bytes 262144 | tf_op jit(solution)/shard_map/all_to_all | solution.py:261
  30.0 0.0 copy-done.2
  30.0 0.0 copy-done.3
  30.0 0.0 copy-done
  30.0 0.0 copy-done.1
  30.0 0.7 %shard_map.120 = (bf16[1024,128]{1,0:T(8,128)(2,1)S(1)}, bf16[128,512]{1,0:T(8,128)(2,1)S(1)}, f32[128,512]{1,0:T(8,128)S(1)}) custom-call(bf16[512,128]{1,0:T(8,128)(2,1)S(1)} %bitcast.13, f32[128,512]{1,0:T(8,128)S(1)} %get-tuple-element.14.state, f32[128,512]{1,0:T(8,128)S(1)} %get-tuple-element.15.gating, f32[4,128]{1,0:T(4,128)S(1)} %get-tuple-element.16.mask, ...), custom_call_target="tpu_custom_call" | custom-call | tf_op jit(solution)/shard_map/pallas_call | solution.py:241
  30.8 10.3 %all_to_all.22 = bf16[16,64,128]{2,1,0:T(8,128)(2,1)S(1)} all-to-all(bf16[16,64,128]{2,1,0:T(8,128)(2,1)S(1)} %bitcast.15), channel_id=1, replica_groups={{0,1,2,3,4,5,6,7,8,9,10,11,12,13,14,15},{16,17,18,19,20,21,22,23,24,25,..., dimensions={0} | all-to-all | bytes 524288 | tf_op jit(solution)/shard_map/all_to_all | solution.py:261
  41.1 0.3 shard_map.121
  41.4 12.3 %all_to_all.23 = bf16[32,32,128]{2,1,0:T(8,128)(2,1)S(1)} all-to-all(bf16[32,32,128]{2,1,0:T(8,128)(2,1)S(1)} %bitcast.12), channel_id=1, replica_groups=mesh['grp'=4,'blk'=8] {'grp','blk'}, dimensions={0} | all-to-all | bytes 524288 | tf_op jit(solution)/shard_map/all_to_all | solution.py:261
  53.7 1.0 %shard_map.122 = bf16[4,128,128]{2,1,0:T(8,128)(2,1)} custom-call(bf16[1024,128]{1,0:T(8,128)(2,1)S(1)} %bitcast.9, bf16[128,512]{1,0:T(8,128)(2,1)S(1)} %get-tuple-element.19.state, f32[128,512]{1,0:T(8,128)S(1)} %get-tuple-element.20.gating, f32[128,8]{1,0:T(8,128)S(1)} %get-tuple-element.17.turned, bf16[2,128,128]{2,1,0:T(8,128)(2,1)S(1)} %copy-done.2), custom_call_target="tpu_custom_call" | custom-call | tf_op jit(solution)/shard_map/pallas_call | solution.py:241
Async XLA Ops:
  19.4 10.7 %copy-start.2 = (bf16[2,128,128]{2,1,0:T(8,128)(2,1)S(1)}, bf16[2,128,128]{2,1,0:T(8,128)(2,1)}, u32[]{:S(2)}) copy-start(bf16[2,128,128]{2,1,0:T(8,128)(2,1)} %weight_o.3) | copy-start | bytes 196612
  19.4 10.7 %copy-start.3 = (bf16[2,128,128]{2,1,0:T(8,128)(2,1)S(1)}, bf16[2,128,128]{2,1,0:T(8,128)(2,1)}, u32[]{:S(2)}) copy-start(bf16[2,128,128]{2,1,0:T(8,128)(2,1)} %gate.1) | copy-start | bytes 196612
  19.6 10.4 %copy-start = (bf16[2,128,256]{2,1,0:T(8,128)(2,1)S(1)}, bf16[2,128,256]{2,1,0:T(8,128)(2,1)}, u32[]{:S(2)}) copy-start(bf16[2,128,256]{2,1,0:T(8,128)(2,1)} %left.1) | copy-start | bytes 393220
  19.6 10.4 %copy-start.1 = (bf16[2,128,256]{2,1,0:T(8,128)(2,1)S(1)}, bf16[2,128,256]{2,1,0:T(8,128)(2,1)}, u32[]{:S(2)}) copy-start(bf16[2,128,256]{2,1,0:T(8,128)(2,1)} %right.1) | copy-start | bytes 393220

commit v8 on v6

--- a/solution.py
+++ b/solution.py
@@ -213,7 +213,7 @@
     pack(e32, out)
 
 
-def end_kernel(y, state, gating, turned, weight_o, out, y32):
+def end_kernel(y, state, gating, turned, weight_o, out, y32, ready, written):
     row_count, columns, channels = out.shape
     gain_o, bias_o = spread(turned[:, 1:2]), spread(turned[:, 3:4])
     weight = jnp.transpose(weight_o[1] * 0.5)
@@ -222,10 +222,14 @@
     stored = (state[...].astype(F32) + gating[...] * update).astype(BF16)
     for row in range(row_count):
         lanes = slice(row * columns, (row + 1) * columns)
-        out[row] = jnp.transpose(stored[:, lanes])
-
-
-def call(kernel, shapes, scratch, semaphores=0, far_in=False):
+        ready[row] = jnp.transpose(stored[:, lanes])
+        if row % 1 == 1 - 1:
+            done = pl.ds(row - 1 + 1, 1)
+            pltpu.make_async_copy(ready.at[done], out.at[done], written.at[0]).start()
+    pltpu.make_async_copy(ready, out, written.at[0]).wait()
+
+
+def call(kernel, shapes, scratch, semaphores=0, far_in=False, far_out=False):
     near = pl.BlockSpec(memory_space=pltpu.VMEM)
     far = pl.BlockSpec(memory_space=pltpu.HBM)
 
@@ -236,7 +240,7 @@
             kernel,
             out_shape=[jax.ShapeDtypeStruct(*s) for s in shapes],
             in_specs=[far if far_in else near] * len(operands),
-            out_specs=[near] * len(shapes),
+            out_specs=[far if far_out else near] * len(shapes),
             scratch_shapes=[pltpu.VMEM(*s) for s in scratch]
             + [pltpu.SemaphoreType.DMA((semaphores,))] * (semaphores > 0),
             compiler_params=pltpu.CompilerParams(vmem_limit_bytes=16 << 20),
@@ -314,7 +318,9 @@
     return call(
         end_kernel,
         [(pair_repr.shape, BF16)],
-        [tall(prod)],
+        [tall(prod), (pair_repr.shape, BF16)],
+        semaphores=1,
+        far_out=True,
     )(back, state, gating, turned, output_weight)[0]
 
 

time: 55.1 us -> 55 us (level)
  no operation moved by 1% of the time
where the time goes in v8:
time: 55 us; the launch traced here: 54.8 us
  blocking collectives  50.9 us (93%)
  Pallas kernels  3.82 us (7%)
    all_to_all x4, blocking collectives, exchange(): lax.all_to_all(rows.reshape(devices, count // devices, columns), AXES, sp...  50.9 us
    pallas_call x5, Pallas kernels, run(): pl.pallas_call(kernel, out_shape=[jax.ShapeDtypeStruct(*s) for s in shape...  3.82 us

profile of v8, /device:TPU:0, one launch (start us, length us, event | category | flops | bytes accessed | tf_op | source)
XLA Modules:
  0.0 54.8 jit_solution(3323162760229113969)
XLA Ops:
  0.0 1.6 %shard_map.118 = (bf16[1024,128]{1,0:T(8,128)(2,1)S(1)}, f32[128,512]{1,0:T(8,128)S(1)}, f32[128,512]{1,0:T(8,128)S(1)}, f32[4,128]{1,0:T(4,128)S(1)}, f32[128,8]{1,0:T(8,128)S(1)}) custom-call(bf16[4,128,128]{2,1,0:T(8,128)(2,1)} %pair_h.1, s32[4,128]{1,0:T(4,128)} %mask_h.1, s32[1,128]{1,0:T(1,128)} %bitcast.17, f32[2,128]{1,0:T(2,128)} %embed_h.1, ...), custom_call_target="tpu_custom_call" | custom-call | tf_op jit(solution)/shard_map/pallas_call | solution.py:239
  1.6 17.7 %all_to_all.20 = bf16[32,32,128]{2,1,0:T(8,128)(2,1)S(1)} all-to-all(bf16[32,32,128]{2,1,0:T(8,128)(2,1)S(1)} %bitcast.16), channel_id=1, replica_groups=mesh['grp'=4,'blk'=8] {'grp','blk'}, dimensions={0} | all-to-all | bytes 524288 | tf_op jit(solution)/shard_map/all_to_all | solution.py:255
  19.4 0.0 copy-start.2
  19.4 0.0 copy-start.3
  19.4 0.2 shard_map.119
  19.6 0.0 copy-start
  19.6 0.0 copy-start.1
  19.6 10.4 %all_to_all.21 = bf16[32,16,128]{2,1,0:T(8,128)(2,1)S(1)} all-to-all(bf16[32,16,128]{2,1,0:T(8,128)(2,1)S(1)} %bitcast.12), channel_id=1, replica_groups=mesh['grp'=4,'blk'=8] {'grp','blk'}, dimensions={0} | all-to-all | bytes 262144 | tf_op jit(solution)/shard_map/all_to_all | solution.py:255
  30.0 0.0 copy-done.2
  30.0 0.0 copy-done.3
  30.0 0.0 copy-done
  30.0 0.0 copy-done.1
  30.0 0.7 %shard_map.120 = (bf16[1024,128]{1,0:T(8,128)(2,1)S(1)}, bf16[128,512]{1,0:T(8,128)(2,1)S(1)}, f32[128,512]{1,0:T(8,128)S(1)}) custom-call(bf16[512,128]{1,0:T(8,128)(2,1)S(1)} %bitcast.11, f32[128,512]{1,0:T(8,128)S(1)} %get-tuple-element.14.state, f32[128,512]{1,0:T(8,128)S(1)} %get-tuple-element.15.gating, f32[4,128]{1,0:T(4,128)S(1)} %get-tuple-element.16.mask, ...), custom_call_target="tpu_custom_call" | custom-call | tf_op jit(solution)/shard_map/pallas_call | solution.py:239
  30.8 12.3 %all_to_all.22 = bf16[32,32,128]{2,1,0:T(8,128)(2,1)S(1)} all-to-all(bf16[32,32,128]{2,1,0:T(8,128)(2,1)S(1)} %bitcast.15), channel_id=1, replica_groups=mesh['grp'=4,'blk'=8] {'grp','blk'}, dimensions={0} | all-to-all | bytes 524288 | tf_op jit(solution)/shard_map/all_to_all | solution.py:255
  43.1 0.2 shard_map.121
  43.4 10.4 %all_to_all.23 = bf16[32,16,128]{2,1,0:T(8,128)(2,1)S(1)} all-to-all(bf16[32,16,128]{2,1,0:T(8,128)(2,1)S(1)} %bitcast.13), channel_id=1, replica_groups=mesh['grp'=4,'blk'=8] {'grp','blk'}, dimensions={0} | all-to-all | bytes 262144 | tf_op jit(solution)/shard_map/all_to_all | solution.py:255
  53.8 1.0 %shard_map.122 = bf16[4,128,128]{2,1,0:T(8,128)(2,1)} custom-call(bf16[512,128]{1,0:T(8,128)(2,1)S(1)} %bitcast.14, bf16[128,512]{1,0:T(8,128)(2,1)S(1)} %get-tuple-element.19.state, f32[128,512]{1,0:T(8,128)S(1)} %get-tuple-element.20.gating, f32[128,8]{1,0:T(8,128)S(1)} %get-tuple-element.17.turned, bf16[2,128,128]{2,1,0:T(8,128)(2,1)S(1)} %copy-done.2), custom_call_target="tpu_custom_call" | custom-call | tf_op jit(solution)/shard_map/pallas_call | solution.py:239
Async XLA Ops:
  19.4 10.7 %copy-start.2 = (bf16[2,128,128]{2,1,0:T(8,128)(2,1)S(1)}, bf16[2,128,128]{2,1,0:T(8,128)(2,1)}, u32[]{:S(2)}) copy-start(bf16[2,128,128]{2,1,0:T(8,128)(2,1)} %weight_o.3) | copy-start | bytes 196612
  19.4 10.7 %copy-start.3 = (bf16[2,128,128]{2,1,0:T(8,128)(2,1)S(1)}, bf16[2,128,128]{2,1,0:T(8,128)(2,1)}, u32[]{:S(2)}) copy-start(bf16[2,128,128]{2,1,0:T(8,128)(2,1)} %gate.1) | copy-start | bytes 196612
  19.6 10.4 %copy-start = (bf16[2,128,256]{2,1,0:T(8,128)(2,1)S(1)}, bf16[2,128,256]{2,1,0:T(8,128)(2,1)}, u32[]{:S(2)}) copy-start(bf16[2,128,256]{2,1,0:T(8,128)(2,1)} %left.1) | copy-start | bytes 393220
  19.6 10.4 %copy-start.1 = (bf16[2,128,256]{2,1,0:T(8,128)(2,1)S(1)}, bf16[2,128,256]{2,1,0:T(8,128)(2,1)}, u32[]{:S(2)}) copy-start(bf16[2,128,256]{2,1,0:T(8,128)(2,1)} %right.1) | copy-start | bytes 393220

commit v9 on v6

--- a/solution.py
+++ b/solution.py
@@ -35,10 +35,10 @@
     return jnp.transpose(jnp.concatenate(scaled, axis=1))
 
 
-def halves(left, right, gate):
+def halves(left, right):
     hidden = left.shape[-1] // 2
     return [
-        left[..., :hidden], left[..., hidden:], right[..., :hidden], right[..., hidden:], gate
+        left[..., :hidden], left[..., hidden:], right[..., :hidden], right[..., hidden:]
     ]
 
 
@@ -74,7 +74,7 @@
         out[:, part * LANES : (part + 1) * LANES] = ref[part].astype(BF16)
 
 
-def project(normed, weights, first, mask, e32, gating):
+def project(normed, weights, first, mask, e32):
     row_count, columns = mask.shape
     hidden = e32.shape[1] // (2 * row_count)
     projected = jnp.dot(weights, normed, preferred_element_type=F32)
@@ -88,12 +88,11 @@
             values = (jnp.tanh(block[low : low + hidden]) + 1.0) * values
             rows = pl.ds(side * row_count + row, hidden, stride=2 * row_count)
             e32[column // LANES, rows, :] = values
-        gating[:, first + at : first + at + LANES] = jnp.tanh(block[4 * hidden :]) + 1.0
 
 
 def start_kernel(
-    pair_h, mask_h, chain_h, embed_h, gain_h, bias_h, gain_oh, bias_oh, left_h, right_h, gate_h,
-    out, state, gating, mask_out, columns_out,
+    pair_h, mask_h, chain_h, embed_h, gain_h, bias_h, gain_oh, bias_oh, left_h, right_h,
+    out, state, normed_out, mask_out, columns_out,
     pair, mask, chain, small, weights, e32, rows, arrived,
 ):
     row_count, columns, channels = pair.shape
@@ -102,7 +101,7 @@
     moves += [(source, small.at[place], 1) for place, source in enumerate(smalls)]
     moves += [(chain_h, chain, 2)]
     hidden = weights.shape[2]
-    for place, source in enumerate((left_h, left_h, right_h, right_h, gate_h)):
+    for place, source in enumerate((left_h, left_h, right_h, right_h)):
         lanes = pl.ds(place % 2 * hidden, hidden)
         moves += [(source.at[0, :, lanes], weights.at[place], 3)]
     moves += [(mask_h, mask, 4)]
@@ -146,7 +145,8 @@
     turned = turn_all([weights[place] for place in range(weights.shape[0])])
     for place in range(0, len(normed), 2):
         pair_of = jnp.concatenate(normed[place : place + 2], axis=1)
-        project(pair_of, turned, place * LANES, mask_out, e32, gating)
+        normed_out[:, place * LANES : (place + 2) * LANES] = pair_of
+        project(pair_of, turned, place * LANES, mask_out, e32)
     pack(e32, out)
 
 
@@ -156,7 +156,9 @@
     return firsts, jnp.where(upper, pltpu.roll(low, half, 1), high)
 
 
-def product_kernel(incoming, devices, x, out):
+def product_kernel(block_index, devices, x, normed, gate, out, gating):
+    weight = jnp.transpose(gate[block_index] * 0.5)
+    gating[...] = jnp.tanh(jnp.dot(weight, normed[...], preferred_element_type=F32)) + 1.0
     columns = x.shape[1]
     row_count = columns // devices
     per_device = x.shape[0] // (2 * columns)
@@ -167,7 +169,7 @@
         left, right = (side.reshape(columns, columns).astype(BF16) for side in sides)
         products.append(
             lax.dot_general(
-                left, right, ON_SUBLANES if incoming else ON_LANES, preferred_element_type=F32
+                left, right, ON_SUBLANES if block_index else ON_LANES, preferred_element_type=F32
             ).reshape(devices // 2, 2 * row_count, columns)
         )
     if per_device == 1:
@@ -193,14 +195,14 @@
 
 
 def middle_kernel(
-    y, state, gating, mask, turned, weight_o, left, right, gate,
-    out, state_out, gating_out, y32, e32,
+    y, state, gating, mask, turned, weight_o, left, right,
+    out, state_out, normed_out, y32, e32,
 ):
     row_count, columns = mask.shape
     gain_o, bias_o = spread(turned[:, 0:1]), spread(turned[:, 2:3])
     gain, bias = spread(turned[:, 5:6]), spread(turned[:, 7:8])
     weight = jnp.transpose(weight_o[0] * 0.5)
-    weights = turn_all(halves(left[1], right[1], gate[1]))
+    weights = turn_all(halves(left[1], right[1]))
     widen(y, y32)
     for at in range(0, row_count * columns, 2 * LANES):
         lanes = slice(at, at + 2 * LANES)
@@ -209,7 +211,9 @@
         state_out[:, lanes] = stored
         values = stored.astype(F32)
         normed = [normalize(values[:, q : q + LANES], gain, bias) for q in (0, LANES)]
-        project(jnp.concatenate(normed, axis=1), weights, at, mask, e32, gating_out)
+        flat = jnp.concatenate(normed, axis=1)
+        normed_out[:, lanes] = flat
+        project(flat, weights, at, mask, e32)
     pack(e32, out)
 
 
@@ -285,32 +289,34 @@
 
     columnar = ((channels, 8), F32)
 
-    sent, state, gating, mask, turned = call(
+    sent, state, normed, mask, turned = call(
         start_kernel,
-        [(edge, BF16), (wide, F32), (wide, F32), (pair_mask.shape, F32), columnar],
+        [(edge, BF16), (wide, F32), (wide, BF16), (pair_mask.shape, F32), columnar],
         [(pair_repr.shape, BF16), (pair_mask.shape, jnp.int32), ((1, columns), jnp.int32)]
-        + [((5, 2, channels), F32), ((5, channels, hidden), BF16), tall(edge), ((8, channels), F32)],
+        + [((5, 2, channels), F32), ((4, channels, hidden), BF16), tall(edge), ((8, channels), F32)],
         semaphores=5,
         far_in=True,
     )(
         pair_repr, pair_mask, chain_index.reshape(1, -1), entity_embed, input_gain, input_bias,
-        output_gain, output_bias, left_weight, right_weight, gate_weight,
+        output_gain, output_bias, left_weight, right_weight,
     )
 
-    def product(rows, incoming):
+    def product(rows, block_index, normed):
         return call(
-            functools.partial(product_kernel, incoming, devices),
-            [(prod, BF16)],
+            functools.partial(product_kernel, block_index, devices),
+            [(prod, BF16), (wide, F32)],
             [],
-        )(rows)[0]
-
-    back = exchange(product(exchange(sent), False))
-    sent, state, gating = call(
+        )(rows, normed, gate_weight)
+
+    back, gating = product(exchange(sent), 0, normed)
+    back = exchange(back)
+    sent, state, normed = call(
         middle_kernel,
-        [(edge, BF16), (wide, BF16), (wide, F32)],
+        [(edge, BF16), (wide, BF16), (wide, BF16)],
         [tall(prod), tall(edge)],
-    )(back, state, gating, mask, turned, output_weight, left_weight, right_weight, gate_weight)
-    back = exchange(product(exchange(sent), True))
+    )(back, state, gating, mask, turned, output_weight, left_weight, right_weight)
+    back, gating = product(exchange(sent), 1, normed)
+    back = exchange(back)
     return call(
         end_kernel,
         [(pair_repr.shape, BF16)],

time: 55.1 us -> 55.1 us (level)
  no operation moved by 1% of the time
where the time goes in v9:
time: 55.1 us; the launch traced here: 54.8 us
  blocking collectives  50.9 us (92%)
  Pallas kernels  3.87 us (7%)
    all_to_all x4, blocking collectives, exchange(): lax.all_to_all(rows.reshape(devices, count // devices, columns), AXES, sp...  50.9 us
    pallas_call x5, Pallas kernels, run(): pl.pallas_call(kernel, out_shape=[jax.ShapeDtypeStruct(*s) for s in shape...  3.87 us

profile of v9, /device:TPU:0, one launch (start us, length us, event | category | flops | bytes accessed | tf_op | source)
XLA Modules:
  0.0 54.8 jit_solution(14502726488868814380)
XLA Ops:
  0.0 1.6 %shard_map.118 = (bf16[1024,128]{1,0:T(8,128)(2,1)S(1)}, f32[128,512]{1,0:T(8,128)S(1)}, bf16[128,512]{1,0:T(8,128)(2,1)S(1)}, f32[4,128]{1,0:T(4,128)S(1)}, f32[128,8]{1,0:T(8,128)S(1)}) custom-call(bf16[4,128,128]{2,1,0:T(8,128)(2,1)} %pair_h.1, s32[4,128]{1,0:T(4,128)} %mask_h.1, s32[1,128]{1,0:T(1,128)} %bitcast.17, f32[2,128]{1,0:T(2,128)} %embed_h.1, ...), custom_call_target="tpu_custom_call" | custom-call | tf_op jit(solution)/shard_map/pallas_call | solution.py:239
  1.6 0.0 copy-start.2
  1.6 17.7 %all_to_all.20 = bf16[32,32,128]{2,1,0:T(8,128)(2,1)S(1)} all-to-all(bf16[32,32,128]{2,1,0:T(8,128)(2,1)S(1)} %bitcast.14), channel_id=1, replica_groups=mesh['grp'=4,'blk'=8] {'grp','blk'}, dimensions={0} | all-to-all | bytes 524288 | tf_op jit(solution)/shard_map/all_to_all | solution.py:255
  19.3 0.0 copy-done.2
  19.3 0.0 copy-start.3
  19.3 0.3 shard_map.119
  19.6 0.0 copy-start
  19.6 0.0 copy-start.1
  19.6 10.4 %all_to_all.21 = bf16[32,16,128]{2,1,0:T(8,128)(2,1)S(1)} all-to-all(bf16[32,16,128]{2,1,0:T(8,128)(2,1)S(1)} %bitcast.15), channel_id=1, replica_groups=mesh['grp'=4,'blk'=8] {'grp','blk'}, dimensions={0} | all-to-all | bytes 262144 | tf_op jit(solution)/shard_map/all_to_all | solution.py:255
  30.1 0.0 copy-done.3
  30.1 0.0 copy-done
  30.1 0.0 copy-done.1
  30.1 0.7 %shard_map.120 = (bf16[1024,128]{1,0:T(8,128)(2,1)S(1)}, bf16[128,512]{1,0:T(8,128)(2,1)S(1)}, bf16[128,512]{1,0:T(8,128)(2,1)S(1)}) custom-call(bf16[512,128]{1,0:T(8,128)(2,1)S(1)} %bitcast.12, f32[128,512]{1,0:T(8,128)S(1)} %get-tuple-element.20.state, f32[128,512]{1,0:T(8,128)S(1)} %get-tuple-element.21.gating, f32[4,128]{1,0:T(4,128)S(1)} %get-tuple-element.22.mask, ...), custom_call_target="tpu_custom_call" | custom-call | tf_op jit(solution)/shard_map/pallas_call | solution.py:239
  30.8 12.3 %all_to_all.22 = bf16[32,32,128]{2,1,0:T(8,128)(2,1)S(1)} all-to-all(bf16[32,32,128]{2,1,0:T(8,128)(2,1)S(1)} %bitcast.13), channel_id=1, replica_groups=mesh['grp'=4,'blk'=8] {'grp','blk'}, dimensions={0} | all-to-all | bytes 524288 | tf_op jit(solution)/shard_map/all_to_all | solution.py:255
  43.1 0.3 shard_map.121
  43.4 10.4 %all_to_all.23 = bf16[32,16,128]{2,1,0:T(8,128)(2,1)S(1)} all-to-all(bf16[32,16,128]{2,1,0:T(8,128)(2,1)S(1)} %bitcast.16), channel_id=1, replica_groups=mesh['grp'=4,'blk'=8] {'grp','blk'}, dimensions={0} | all-to-all | bytes 262144 | tf_op jit(solution)/shard_map/all_to_all | solution.py:255
  53.8 1.0 %shard_map.122 = bf16[4,128,128]{2,1,0:T(8,128)(2,1)} custom-call(bf16[512,128]{1,0:T(8,128)(2,1)S(1)} %bitcast.11, bf16[128,512]{1,0:T(8,128)(2,1)S(1)} %get-tuple-element.27.state, f32[128,512]{1,0:T(8,128)S(1)} %get-tuple-element.28.gating, f32[128,8]{1,0:T(8,128)S(1)} %get-tuple-element.23.turned, bf16[2,128,128]{2,1,0:T(8,128)(2,1)S(1)} %copy-done.3), custom_call_target="tpu_custom_call" | custom-call | tf_op jit(solution)/shard_map/pallas_call | solution.py:239
Async XLA Ops:
  1.6 17.7 %copy-start.2 = (bf16[2,128,128]{2,1,0:T(8,128)(2,1)S(1)}, bf16[2,128,128]{2,1,0:T(8,128)(2,1)}, u32[]{:S(2)}) copy-start(bf16[2,128,128]{2,1,0:T(8,128)(2,1)} %gate.3) | copy-start | bytes 196612
  19.3 10.7 %copy-start.3 = (bf16[2,128,128]{2,1,0:T(8,128)(2,1)S(1)}, bf16[2,128,128]{2,1,0:T(8,128)(2,1)}, u32[]{:S(2)}) copy-start(bf16[2,128,128]{2,1,0:T(8,128)(2,1)} %weight_o.3) | copy-start | bytes 196612
  19.6 10.4 %copy-start = (bf16[2,128,256]{2,1,0:T(8,128)(2,1)S(1)}, bf16[2,128,256]{2,1,0:T(8,128)(2,1)}, u32[]{:S(2)}) copy-start(bf16[2,128,256]{2,1,0:T(8,128)(2,1)} %left.1) | copy-start | bytes 393220
  19.6 10.4 %copy-start.1 = (bf16[2,128,256]{2,1,0:T(8,128)(2,1)S(1)}, bf16[2,128,256]{2,1,0:T(8,128)(2,1)}, u32[]{:S(2)}) copy-start(bf16[2,128,256]{2,1,0:T(8,128)(2,1)} %right.1) | copy-start | bytes 393220

commit v10 on v9

--- a/solution.py
+++ b/solution.py
@@ -217,7 +217,7 @@
     pack(e32, out)
 
 
-def end_kernel(y, state, gating, turned, weight_o, out, y32):
+def end_kernel(y, state, gating, turned, weight_o, out, y32, ready, written):
     row_count, columns, channels = out.shape
     gain_o, bias_o = spread(turned[:, 1:2]), spread(turned[:, 3:4])
     weight = jnp.transpose(weight_o[1] * 0.5)
@@ -226,10 +226,14 @@
     stored = (state[...].astype(F32) + gating[...] * update).astype(BF16)
     for row in range(row_count):
         lanes = slice(row * columns, (row + 1) * columns)
-        out[row] = jnp.transpose(stored[:, lanes])
-
-
-def call(kernel, shapes, scratch, semaphores=0, far_in=False):
+        ready[row] = jnp.transpose(stored[:, lanes])
+        if row % 1 == 1 - 1:
+            done = pl.ds(row - 1 + 1, 1)
+            pltpu.make_async_copy(ready.at[done], out.at[done], written.at[0]).start()
+    pltpu.make_async_copy(ready, out, written.at[0]).wait()
+
+
+def call(kernel, shapes, scratch, semaphores=0, far_in=False, far_out=False):
     near = pl.BlockSpec(memory_space=pltpu.VMEM)
     far = pl.BlockSpec(memory_space=pltpu.HBM)
 
@@ -240,7 +244,7 @@
             kernel,
             out_shape=[jax.ShapeDtypeStruct(*s) for s in shapes],
             in_specs=[far if far_in else near] * len(operands),
-            out_specs=[near] * len(shapes),
+            out_specs=[far if far_out else near] * len(shapes),
             scratch_shapes=[pltpu.VMEM(*s) for s in scratch]
             + [pltpu.SemaphoreType.DMA((semaphores,))] * (semaphores > 0),
             compiler_params=pltpu.CompilerParams(vmem_limit_bytes=16 << 20),
@@ -320,7 +324,9 @@
     return call(
         end_kernel,
         [(pair_repr.shape, BF16)],
-        [tall(prod)],
+        [tall(prod), (pair_repr.shape, BF16)],
+        semaphores=1,
+        far_out=True,
     )(back, state, gating, turned, output_weight)[0]
 
 

time: 55.1 us -> 55.1 us (level)
  no operation moved by 1% of the time
where the time goes in v10:
time: 55.1 us; the launch traced here: 54.8 us
  blocking collectives  50.9 us (92%)
  Pallas kernels  3.85 us (7%)
    all_to_all x4, blocking collectives, exchange(): lax.all_to_all(rows.reshape(devices, count // devices, columns), AXES, sp...  50.9 us
    pallas_call x5, Pallas kernels, run(): pl.pallas_call(kernel, out_shape=[jax.ShapeDtypeStruct(*s) for s in shape...  3.85 us

profile of v10, /device:TPU:0, one launch (start us, length us, event | category | flops | bytes accessed | tf_op | source)
XLA Modules:
  0.0 54.8 jit_solution(4261923274403829028)
XLA Ops:
  0.0 1.6 %shard_map.118 = (bf16[1024,128]{1,0:T(8,128)(2,1)S(1)}, f32[128,512]{1,0:T(8,128)S(1)}, bf16[128,512]{1,0:T(8,128)(2,1)S(1)}, f32[4,128]{1,0:T(4,128)S(1)}, f32[128,8]{1,0:T(8,128)S(1)}) custom-call(bf16[4,128,128]{2,1,0:T(8,128)(2,1)} %pair_h.1, s32[4,128]{1,0:T(4,128)} %mask_h.1, s32[1,128]{1,0:T(1,128)} %bitcast.17, f32[2,128]{1,0:T(2,128)} %embed_h.1, ...), custom_call_target="tpu_custom_call" | custom-call | tf_op jit(solution)/shard_map/pallas_call | solution.py:243
  1.6 0.0 copy-start.2
  1.6 17.7 %all_to_all.20 = bf16[32,32,128]{2,1,0:T(8,128)(2,1)S(1)} all-to-all(bf16[32,32,128]{2,1,0:T(8,128)(2,1)S(1)} %bitcast.14), channel_id=1, replica_groups=mesh['grp'=4,'blk'=8] {'grp','blk'}, dimensions={0} | all-to-all | bytes 524288 | tf_op jit(solution)/shard_map/all_to_all | solution.py:259
  19.3 0.0 copy-done.2
  19.3 0.0 copy-start.3
  19.3 0.3 shard_map.119
  19.6 0.0 copy-start
  19.6 0.0 copy-start.1
  19.6 10.4 %all_to_all.21 = bf16[32,16,128]{2,1,0:T(8,128)(2,1)S(1)} all-to-all(bf16[32,16,128]{2,1,0:T(8,128)(2,1)S(1)} %bitcast.15), channel_id=1, replica_groups=mesh['grp'=4,'blk'=8] {'grp','blk'}, dimensions={0} | all-to-all | bytes 262144 | tf_op jit(solution)/shard_map/all_to_all | solution.py:259
  30.1 0.0 copy-done.3
  30.1 0.0 copy-done
  30.1 0.0 copy-done.1
  30.1 0.7 %shard_map.120 = (bf16[1024,128]{1,0:T(8,128)(2,1)S(1)}, bf16[128,512]{1,0:T(8,128)(2,1)S(1)}, bf16[128,512]{1,0:T(8,128)(2,1)S(1)}) custom-call(bf16[512,128]{1,0:T(8,128)(2,1)S(1)} %bitcast.12, f32[128,512]{1,0:T(8,128)S(1)} %get-tuple-element.20.state, f32[128,512]{1,0:T(8,128)S(1)} %get-tuple-element.21.gating, f32[4,128]{1,0:T(4,128)S(1)} %get-tuple-element.22.mask, ...), custom_call_target="tpu_custom_call" | custom-call | tf_op jit(solution)/shard_map/pallas_call | solution.py:243
  30.8 12.3 %all_to_all.22 = bf16[32,32,128]{2,1,0:T(8,128)(2,1)S(1)} all-to-all(bf16[32,32,128]{2,1,0:T(8,128)(2,1)S(1)} %bitcast.13), channel_id=1, replica_groups=mesh['grp'=4,'blk'=8] {'grp','blk'}, dimensions={0} | all-to-all | bytes 524288 | tf_op jit(solution)/shard_map/all_to_all | solution.py:259
  43.1 0.3 shard_map.121
  43.4 10.4 %all_to_all.23 = bf16[32,16,128]{2,1,0:T(8,128)(2,1)S(1)} all-to-all(bf16[32,16,128]{2,1,0:T(8,128)(2,1)S(1)} %bitcast.16), channel_id=1, replica_groups=mesh['grp'=4,'blk'=8] {'grp','blk'}, dimensions={0} | all-to-all | bytes 262144 | tf_op jit(solution)/shard_map/all_to_all | solution.py:259
  53.8 1.0 %shard_map.122 = bf16[4,128,128]{2,1,0:T(8,128)(2,1)} custom-call(bf16[512,128]{1,0:T(8,128)(2,1)S(1)} %bitcast.11, bf16[128,512]{1,0:T(8,128)(2,1)S(1)} %get-tuple-element.27.state, f32[128,512]{1,0:T(8,128)S(1)} %get-tuple-element.28.gating, f32[128,8]{1,0:T(8,128)S(1)} %get-tuple-element.23.turned, bf16[2,128,128]{2,1,0:T(8,128)(2,1)S(1)} %copy-done.3), custom_call_target="tpu_custom_call" | custom-call | tf_op jit(solution)/shard_map/pallas_call | solution.py:243
Async XLA Ops:
  1.6 17.7 %copy-start.2 = (bf16[2,128,128]{2,1,0:T(8,128)(2,1)S(1)}, bf16[2,128,128]{2,1,0:T(8,128)(2,1)}, u32[]{:S(2)}) copy-start(bf16[2,128,128]{2,1,0:T(8,128)(2,1)} %gate.3) | copy-start | bytes 196612
  19.3 10.7 %copy-start.3 = (bf16[2,128,128]{2,1,0:T(8,128)(2,1)S(1)}, bf16[2,128,128]{2,1,0:T(8,128)(2,1)}, u32[]{:S(2)}) copy-start(bf16[2,128,128]{2,1,0:T(8,128)(2,1)} %weight_o.3) | copy-start | bytes 196612
  19.6 10.4 %copy-start = (bf16[2,128,256]{2,1,0:T(8,128)(2,1)S(1)}, bf16[2,128,256]{2,1,0:T(8,128)(2,1)}, u32[]{:S(2)}) copy-start(bf16[2,128,256]{2,1,0:T(8,128)(2,1)} %left.1) | copy-start | bytes 393220
  19.6 10.4 %copy-start.1 = (bf16[2,128,256]{2,1,0:T(8,128)(2,1)S(1)}, bf16[2,128,256]{2,1,0:T(8,128)(2,1)}, u32[]{:S(2)}) copy-start(bf16[2,128,256]{2,1,0:T(8,128)(2,1)} %right.1) | copy-start | bytes 393220
